TPU v7x, 32 devices: a whole 2x2x4 slice. The times are simulated.
32 devices in a mesh: dp: 4 (over y, x), seq: 8 (over z, core).
Axes of the slice: x: 2, y: 2, z: 4, core: 2. Of those that a mesh axis runs over, the one named last changes fastest.
Arguments:
- stream: bfloat16 [4, 1024, 512], P('dp', 'seq'), may hold values from -6 to 6
- byte_ids: int32 [4, 1024], P('dp', 'seq'), may hold values from 0 to 255
- cotangent: bfloat16 [4, 1024, 512], P('dp', 'seq'), may hold values from -6 to 6
- embed_flat: bfloat16 [131072], P(('dp', 'seq')), may hold values from -6 to 6
- qkv_flat: bfloat16 [786432], P(('dp', 'seq')), may hold values from -0.25 to 0.25
- out_flat: bfloat16 [262144], P(('dp', 'seq')), may hold values from -6 to 6
- up_flat: bfloat16 [1048576], P(('dp', 'seq')), may hold values from -0.25 to 0.25
- down_flat: bfloat16 [1048576], P(('dp', 'seq')), may hold values from -0.125 to 0.125
- gains: bfloat16 [1024], P(('dp', 'seq')), may hold values from 0.5 to 1.5
- norm_shifts: bfloat16 [1024], P(('dp', 'seq')), may hold values from -2 to 2
- out_shifts: bfloat16 [1024], P(('dp', 'seq')), may hold values from -2 to 2
- up_bias: bfloat16 [2048], P(('dp', 'seq')), may hold values from -2 to 2
- rel_bias: bfloat16 [256], P(('dp', 'seq')), may hold values from -4 to 4
Outputs:
- activations: bfloat16 [4, 1024, 512], P('dp', 'seq')
- grad_stream: bfloat16 [4, 1024, 512], P('dp', 'seq')
- grad_embed: float32 [131072], P(('dp', 'seq'))
- grad_qkv: float32 [786432], P(('dp', 'seq'))
- grad_out_weight: float32 [262144], P(('dp', 'seq'))
- grad_up: float32 [1048576], P(('dp', 'seq'))
- grad_down: float32 [1048576], P(('dp', 'seq'))
- grad_gains: float32 [1024], P(('dp', 'seq'))
- grad_norm_shifts: float32 [1024], P(('dp', 'seq'))
- grad_out_shifts: float32 [1024], P(('dp', 'seq'))
- grad_up_bias: float32 [2048], P(('dp', 'seq'))
- grad_rel: float32 [256], P(('dp', 'seq'))
All inputs are finite; a program needn't handle non-finite values.
Results may differ from a plain program's by a relative error of at most 0.01.
Values may be sent and summed in bfloat16 or wider, within the bound.
A program may use at most 192 MiB of HBM per device.

v0:
```python
import jax
import jax.numpy as jnp
from jax import lax
from jax.sharding import PartitionSpec as P

D = 512
HEADS = 8
HEAD_DIM = 64
FF = 2048
VOCAB = 256
BLOCK = 256
BUCKETS = 32


EPSILON = 1e-05
SCALING = 0.125
MASKED = -1e30


def layer_norm(hidden, gain_row, shift_row):
    centered = hidden - jnp.mean(hidden, axis=-1, keepdims=True)
    spread = jnp.mean(centered * centered, axis=-1, keepdims=True)
    return centered * lax.rsqrt(spread + EPSILON) * gain_row + shift_row


def gelu_exact(values):
    return jax.nn.gelu(values, approximate=False)


def unpack(gathered):
    embed, w_qkv, w_out, w_up, w_down, gain_flat, norm_flat, out_flat, bias_flat, rel_flat = (
        gathered
    )
    return (
        embed.reshape(VOCAB, D),
        w_qkv.reshape(D, 3 * D),
        w_out.reshape(D, D),
        w_up.reshape(D, FF),
        w_down.reshape(FF, D),
        gain_flat.astype(jnp.float32).reshape(2, D),
        norm_flat.astype(jnp.float32).reshape(2, D),
        out_flat.astype(jnp.float32).reshape(2, D),
        bias_flat.astype(jnp.float32),
        rel_flat.astype(jnp.float32).reshape(HEADS, BUCKETS),
    )


def block_terms(rel_table, row_first, row_count, key_first, key_count):
    row_blocks = max(row_count // BLOCK, 1)
    key_blocks = max(key_count // BLOCK, 1)
    row_ids = row_first // BLOCK + jnp.arange(row_blocks, dtype=jnp.int32)
    key_ids = key_first // BLOCK + jnp.arange(key_blocks, dtype=jnp.int32)
    distance = row_ids[:, None] - key_ids[None, :]
    allowed = distance >= 0
    bucket = jnp.clip(distance, 0, BUCKETS - 1)
    selector = (bucket[:, :, None] == jnp.arange(BUCKETS, dtype=jnp.int32)[None, None, :]).astype(
        jnp.float32
    )
    bias_tiles = jnp.einsum("abn,hn->hab", selector, rel_table, precision=lax.Precision.HIGHEST)
    return (bias_tiles, allowed, selector)


def score_tile(query_heads, key_heads, bias_tiles, allowed):
    row_count = query_heads.shape[0]
    key_count = key_heads.shape[0]
    raw_scores = (
        jnp.einsum("qhd,khd->hqk", query_heads, key_heads, preferred_element_type=jnp.float32)
        * SCALING
    )
    row_blocks = bias_tiles.shape[1]
    key_blocks = bias_tiles.shape[2]
    tiled = raw_scores.reshape(
        HEADS, row_blocks, row_count // row_blocks, key_blocks, key_count // key_blocks
    )
    tiled = tiled + bias_tiles[:, :, None, :, None]
    tiled = jnp.where(allowed[None, :, None, :, None], tiled, MASKED)
    return tiled.reshape(HEADS, row_count, key_count)


def heads_of(rows):
    return rows.reshape(rows.shape[0], HEADS, HEAD_DIM)


def attend(queries, key_rows, value_rows, bias_tiles, allowed):
    local_rows = queries.shape[0]
    scores = score_tile(heads_of(queries), heads_of(key_rows), bias_tiles, allowed)
    row_max = jnp.max(scores, axis=-1, keepdims=True)
    shifted = jnp.exp(scores - row_max)
    row_sum = jnp.sum(shifted, axis=-1, keepdims=True)
    soft_weights = (shifted / row_sum).astype(jnp.bfloat16)
    mixed_heads = jnp.einsum(
        "hqk,khd->qhd", soft_weights, heads_of(value_rows), preferred_element_type=jnp.float32
    )
    return (mixed_heads.reshape(local_rows, D), (row_max + jnp.log(row_sum))[:, :, 0])


def row_back(queries, key_rows, value_rows, log_totals, grad_mixed, bias_tiles, allowed, selector):
    local_rows = queries.shape[0]
    seq_length = key_rows.shape[0]
    query_heads = heads_of(queries)
    key_heads = heads_of(key_rows)
    value_heads = heads_of(value_rows)
    grad_heads = heads_of(grad_mixed)
    scores = score_tile(query_heads, key_heads, bias_tiles, allowed)
    soft_weights = jnp.exp(scores - log_totals[:, :, None])
    grad_weights = jnp.einsum(
        "qhd,khd->hqk", grad_heads, value_heads, preferred_element_type=jnp.float32
    )
    row_inner = jnp.sum(soft_weights * grad_weights, axis=-1)
    grad_scores = soft_weights * (grad_weights - row_inner[:, :, None])
    row_blocks = bias_tiles.shape[1]
    key_blocks = bias_tiles.shape[2]
    tile_sums = jnp.sum(
        grad_scores.reshape(
            HEADS, row_blocks, local_rows // row_blocks, key_blocks, seq_length // key_blocks
        ),
        axis=(2, 4),
    )
    grad_table = jnp.einsum("hab,abn->hn", tile_sums, selector, precision=lax.Precision.HIGHEST)
    scores_low = grad_scores.astype(jnp.bfloat16)
    grad_queries = (
        jnp.einsum("hqk,khd->qhd", scores_low, key_heads, preferred_element_type=jnp.float32)
        * SCALING
    )
    grad_queries = grad_queries.reshape(local_rows, D)
    grad_keys = (
        jnp.einsum("hqk,qhd->khd", scores_low, query_heads, preferred_element_type=jnp.float32)
        * SCALING
    )
    grad_values = jnp.einsum(
        "hqk,qhd->khd",
        soft_weights.astype(jnp.bfloat16),
        grad_heads,
        preferred_element_type=jnp.float32,
    )
    return (
        grad_queries,
        grad_table,
        row_inner,
        grad_keys.reshape(seq_length, D),
        grad_values.reshape(seq_length, D),
    )


def local(
    stream,
    byte_ids,
    cotangent,
    embed_flat,
    qkv_flat,
    out_flat,
    up_flat,
    down_flat,
    gains,
    norm_shifts,
    out_shifts,
    up_bias,
    rel_bias,
):
    seq_count = stream.shape[0]
    local_rows = stream.shape[1]
    seq_length = local_rows * lax.axis_size("seq")
    tokens = seq_count * local_rows
    first_row = lax.axis_index("seq") * local_rows
    owned = (
        embed_flat,
        qkv_flat,
        out_flat,
        up_flat,
        down_flat,
        gains,
        norm_shifts,
        out_shifts,
        up_bias,
        rel_bias,
    )
    gathered = (
        lax.all_gather(owned[0], ("dp", "seq"), axis=0, tiled=True),
        lax.all_gather(owned[1], ("dp", "seq"), axis=0, tiled=True),
        lax.all_gather(owned[2], ("dp", "seq"), axis=0, tiled=True),
        lax.all_gather(owned[3], ("dp", "seq"), axis=0, tiled=True),
        lax.all_gather(owned[4], ("dp", "seq"), axis=0, tiled=True),
        lax.all_gather(owned[5], ("dp", "seq"), axis=0, tiled=True),
        lax.all_gather(owned[6], ("dp", "seq"), axis=0, tiled=True),
        lax.all_gather(owned[7], ("dp", "seq"), axis=0, tiled=True),
        lax.all_gather(owned[8], ("dp", "seq"), axis=0, tiled=True),
        lax.all_gather(owned[9], ("dp", "seq"), axis=0, tiled=True),
    )
    embed, w_qkv, w_out, w_up, w_down, gain_pair, norm_pair, out_pair, bias_up, rel_table = unpack(
        gathered
    )
    picker = byte_ids.reshape(tokens, 1) == jnp.arange(VOCAB, dtype=jnp.int32)[None, :]
    embedded = jnp.dot(picker.astype(jnp.bfloat16), embed, preferred_element_type=jnp.float32)
    start_rows = stream.reshape(tokens, D).astype(jnp.float32) + embedded
    normed_wide, norm_back_one = jax.vjp(layer_norm, start_rows, gain_pair[0], norm_pair[0])
    normed_one = normed_wide.astype(jnp.bfloat16)
    projected = jnp.dot(normed_one, w_qkv, preferred_element_type=jnp.float32).astype(jnp.bfloat16)
    queries = projected[:, :D].reshape(seq_count, local_rows, D)
    key_rows = projected[:, D : 2 * D].reshape(seq_count, local_rows, D)
    value_rows = projected[:, 2 * D :].reshape(seq_count, local_rows, D)
    keys_all, values_all = (
        lax.all_gather(key_rows, "seq", axis=1, tiled=True),
        lax.all_gather(value_rows, "seq", axis=1, tiled=True),
    )
    bias_tiles, allowed, selector = block_terms(rel_table, first_row, local_rows, 0, seq_length)

    def attend_single(operands):
        return attend(operands[0], operands[1], operands[2], bias_tiles, allowed)

    mixed, log_totals = lax.map(attend_single, (queries, keys_all, values_all))
    mixed_low = mixed.reshape(tokens, D).astype(jnp.bfloat16)
    middle = (
        start_rows + jnp.dot(mixed_low, w_out, preferred_element_type=jnp.float32) + out_pair[0]
    )
    normed_mid, norm_back_two = jax.vjp(layer_norm, middle, gain_pair[1], norm_pair[1])
    normed_two = normed_mid.astype(jnp.bfloat16)
    lifted = jnp.dot(normed_two, w_up, preferred_element_type=jnp.float32) + bias_up
    activated, gelu_back = jax.vjp(gelu_exact, lifted)
    active = activated.astype(jnp.bfloat16)
    result = middle + jnp.dot(active, w_down, preferred_element_type=jnp.float32) + out_pair[1]
    gathered_again = (
        lax.all_gather(owned[0], ("dp", "seq"), axis=0, tiled=True),
        lax.all_gather(owned[1], ("dp", "seq"), axis=0, tiled=True),
        lax.all_gather(owned[2], ("dp", "seq"), axis=0, tiled=True),
        lax.all_gather(owned[3], ("dp", "seq"), axis=0, tiled=True),
        lax.all_gather(owned[4], ("dp", "seq"), axis=0, tiled=True),
        lax.all_gather(owned[5], ("dp", "seq"), axis=0, tiled=True),
        lax.all_gather(owned[6], ("dp", "seq"), axis=0, tiled=True),
        lax.all_gather(owned[7], ("dp", "seq"), axis=0, tiled=True),
        lax.all_gather(owned[8], ("dp", "seq"), axis=0, tiled=True),
        lax.all_gather(owned[9], ("dp", "seq"), axis=0, tiled=True),
    )
    embed, w_qkv, w_out, w_up, w_down, gain_pair, norm_pair, out_pair, bias_up, rel_table = unpack(
        gathered_again
    )
    grad_output = cotangent.reshape(tokens, D)
    grad_wide = grad_output.astype(jnp.float32)
    grad_shift_down = jnp.sum(grad_wide, axis=0)
    grad_w_down = jnp.einsum("tf,td->fd", active, grad_output, preferred_element_type=jnp.float32)
    grad_active = jnp.einsum("td,fd->tf", grad_output, w_down, preferred_element_type=jnp.float32)
    (grad_lifted,) = gelu_back(grad_active)
    grad_bias_up = jnp.sum(grad_lifted, axis=0)
    lifted_low = grad_lifted.astype(jnp.bfloat16)
    grad_w_up = jnp.einsum("td,tf->df", normed_two, lifted_low, preferred_element_type=jnp.float32)
    grad_normed_two = jnp.einsum("tf,df->td", lifted_low, w_up, preferred_element_type=jnp.float32)
    grad_mid_norm, grad_gain_two, grad_shift_two = norm_back_two(grad_normed_two)
    grad_middle = grad_wide + grad_mid_norm
    grad_shift_out = jnp.sum(grad_middle, axis=0)
    middle_low = grad_middle.astype(jnp.bfloat16)
    grad_w_out = jnp.einsum("te,td->ed", mixed_low, middle_low, preferred_element_type=jnp.float32)
    grad_mixed = jnp.einsum("td,ed->te", middle_low, w_out, preferred_element_type=jnp.float32)
    grad_mixed = grad_mixed.astype(jnp.bfloat16).reshape(seq_count, local_rows, D)
    keys_all, values_all = (
        lax.all_gather(key_rows, "seq", axis=1, tiled=True),
        lax.all_gather(value_rows, "seq", axis=1, tiled=True),
    )

    def back_with_keys(operands):
        return row_back(
            operands[0],
            operands[1],
            operands[2],
            operands[3],
            operands[4],
            bias_tiles,
            allowed,
            selector,
        )

    grad_queries, grad_tables, unused, grad_keys, grad_values = lax.map(
        back_with_keys, (queries, keys_all, values_all, log_totals, grad_mixed)
    )
    grad_keys, grad_values = (
        lax.psum_scatter(grad_keys, "seq", scatter_dimension=1, tiled=True),
        lax.psum_scatter(grad_values, "seq", scatter_dimension=1, tiled=True),
    )
    grad_table_all = jnp.sum(grad_tables, axis=0)
    grad_projected = jnp.concatenate([grad_queries, grad_keys, grad_values], axis=-1)
    grad_projected = grad_projected.reshape(tokens, 3 * D).astype(jnp.bfloat16)
    grad_w_qkv = jnp.einsum(
        "td,tk->dk", normed_one, grad_projected, preferred_element_type=jnp.float32
    )
    grad_normed_one = jnp.einsum(
        "tk,dk->td", grad_projected, w_qkv, preferred_element_type=jnp.float32
    )
    grad_start_norm, grad_gain_one, grad_shift_one = norm_back_one(grad_normed_one)
    grad_start = grad_middle + grad_start_norm
    grad_embed_local = jnp.einsum(
        "tv,td->vd", picker.astype(jnp.float32), grad_start, precision=lax.Precision.HIGHEST
    )
    local_grads = (
        grad_embed_local.reshape(-1),
        grad_w_qkv.reshape(-1),
        grad_w_out.reshape(-1),
        grad_w_up.reshape(-1),
        grad_w_down.reshape(-1),
        jnp.stack([grad_gain_one, grad_gain_two]).reshape(-1),
        jnp.stack([grad_shift_one, grad_shift_two]).reshape(-1),
        jnp.stack([grad_shift_out, grad_shift_down]).reshape(-1),
        grad_bias_up,
        grad_table_all.reshape(-1),
    )
    summed = (
        lax.psum_scatter(local_grads[0], ("dp", "seq"), scatter_dimension=0, tiled=True),
        lax.psum_scatter(local_grads[1], ("dp", "seq"), scatter_dimension=0, tiled=True),
        lax.psum_scatter(local_grads[2], ("dp", "seq"), scatter_dimension=0, tiled=True),
        lax.psum_scatter(local_grads[3], ("dp", "seq"), scatter_dimension=0, tiled=True),
        lax.psum_scatter(local_grads[4], ("dp", "seq"), scatter_dimension=0, tiled=True),
        lax.psum_scatter(local_grads[5], ("dp", "seq"), scatter_dimension=0, tiled=True),
        lax.psum_scatter(local_grads[6], ("dp", "seq"), scatter_dimension=0, tiled=True),
        lax.psum_scatter(local_grads[7], ("dp", "seq"), scatter_dimension=0, tiled=True),
        lax.psum_scatter(local_grads[8], ("dp", "seq"), scatter_dimension=0, tiled=True),
        lax.psum_scatter(local_grads[9], ("dp", "seq"), scatter_dimension=0, tiled=True),
    )
    return (
        result.reshape(seq_count, local_rows, D).astype(jnp.bfloat16),
        grad_start.reshape(seq_count, local_rows, D).astype(jnp.bfloat16),
        summed[0],
        summed[1],
        summed[2],
        summed[3],
        summed[4],
        summed[5],
        summed[6],
        summed[7],
        summed[8],
        summed[9],
    )


def solution(mesh):
    in_specs = (
        P("dp", "seq", None),
        P("dp", "seq"),
        P("dp", "seq", None),
        P(("dp", "seq")),
        P(("dp", "seq")),
        P(("dp", "seq")),
        P(("dp", "seq")),
        P(("dp", "seq")),
        P(("dp", "seq")),
        P(("dp", "seq")),
        P(("dp", "seq")),
        P(("dp", "seq")),
        P(("dp", "seq")),
    )
    out_specs = (
        P("dp", "seq", None),
        P("dp", "seq", None),
        P(("dp", "seq")),
        P(("dp", "seq")),
        P(("dp", "seq")),
        P(("dp", "seq")),
        P(("dp", "seq")),
        P(("dp", "seq")),
        P(("dp", "seq")),
        P(("dp", "seq")),
        P(("dp", "seq")),
        P(("dp", "seq")),
    )
    return jax.shard_map(local, mesh=mesh, in_specs=in_specs, out_specs=out_specs, check_vma=False)
```

profile of v0, /device:TPU:0, one launch (start us, length us, event | category | flops | bytes accessed | tf_op | source)
XLA Modules:
  0.0 588.8 jit_solution(9069317051377574282)
XLA Ops:
  9.5 44.7 %all_gather.42 = bf16[131072]{0:T(1024)(128)(2,1)S(1)} all-gather(bf16[4096]{0:T(1024)(128)(2,1)} %param.16), channel_id=1, replica_groups=mesh['dp'=4,'seq'=8] {'dp','seq'}, dimensions={0}, use_global_device_ids=true | all-gather | bytes 270336 | tf_op jit(solution)/shard_map/all_gather | solution.py:178
  58.5 37.1 %all-reduce.17 = (bf16[1024]{0:T(1024)(128)(2,1)S(1)}, bf16[1024]{0:T(1024)(128)(2,1)S(1)}, bf16[256]{0:T(256)(128)(2,1)S(1)}, bf16[1024]{0:T(1024)(128)(2,1)S(1)}, bf16[2048]{0:T(1024)(128)(2,1)S(1)}) all-reduce(bf16[1024]{0:T(1024)(128)(2,1)S(1)} %dynamic-update-slice.1, ...), channel_id=1, replica_groups=mesh['dp'=4,'seq'=8] {'dp','seq'}, use_global_device_ids=true, to_apply=%add.1 | all-reduce | flops 5376 | bytes 21504
  97.2 3.3 reshape.371
  102.6 43.2 %all_gather.49 = bf16[262144]{0:T(1024)(128)(2,1)S(1)} all-gather(bf16[8192]{0:T(1024)(128)(2,1)S(1)} %copy-done.24), channel_id=1, replica_groups=mesh['dp'=4,'seq'=8] {'dp','seq'}, dimensions={0}, use_global_device_ids=true | all-gather | bytes 540672 | tf_op jit(solution)/shard_map/all_gather | solution.py:180
  146.8 4.2 reshape.379
  151.0 35.5 %all-gather.12.cloned.1.call-done = bf16[1048576]{0:T(1024)(128)(2,1)} async-done(((bf16[32768]{0:T(1024)(128)(2,1)}), bf16[1048576]{0:T(1024)(128)(2,1)}) %all-gather.12.cloned.1.call-update) | async-done | bytes 2097168 | tf_op jit(solution)/shard_map/all_gather | solution.py:182
  186.5 3.1 reshape.380
  189.6 19.9 %all-gather.16.cloned.1.call-done = bf16[1024,512]{1,0:T(8,128)(2,1)} async-done(((bf16[128,512]{1,0:T(8,128)(2,1)}), bf16[1024,512]{1,0:T(8,128)(2,1)}) %all-gather.16.cloned.1.call-update) | async-done | bytes 1048592 | tf_op jit(solution)/shard_map/all_gather | solution.py:202
  209.5 2.3 copy.43
  211.8 2.1 fusion.64
  214.0 2.0 copy-done
  217.0 16.3 %all-gather.14.cloned.1.call-done = bf16[1024,512]{1,0:T(8,128)(2,1)} async-done(((bf16[128,512]{1,0:T(8,128)(2,1)}), bf16[1024,512]{1,0:T(8,128)(2,1)}) %all-gather.14.cloned.1.call-update) | async-done | bytes 1048592 | tf_op jit(solution)/shard_map/all_gather | solution.py:203
  233.3 2.3 copy.41
  235.6 3.7 fusion.9
  240.0 3.8 multiply_convert_fusion
  243.7 1.5 fusion.66
  245.3 1.5 multiply_reduce_fusion.1
  248.1 4.6 fusion.2
  252.8 3.6 multiply_reduce_fusion
  256.4 1.8 fusion.12
  258.2 1.8 convolution_multiply_fusion
  263.7 2.9 copy.47
  267.3 3.1 copy.48
  271.3 17.0 %reduce-scatter.5.cloned.1.call-done = f32[1,128,512]{1,2,0:T(8,128)} async-done(((f32[1,1024,512]{1,2,0:T(8,128)}), f32[1,128,512]{1,2,0:T(8,128)}) %reduce-scatter.5.cloned.1.call-update) | async-done | bytes 262160 | tf_op jit(solution)/shard_map/reduce_scatter | solution.py:275
  289.3 35.7 %reduce-scatter.3.cloned.1.call-done = f32[1,128,512]{1,2,0:T(8,128)} async-done(((f32[1,1024,512]{1,2,0:T(8,128)}), f32[1,128,512]{1,2,0:T(8,128)}) %reduce-scatter.3.cloned.1.call-update) | async-done | bytes 262160 | tf_op jit(solution)/shard_map/reduce_scatter | solution.py:274
  326.1 2.8 multiply_reduce_fusion.2
  332.0 1.9 reshape.384
  336.9 39.8 %all-reduce.15 = (f32[1024]{0:T(1024)S(1)}, f32[1024]{0:T(1024)S(1)}, f32[1024]{0:T(1024)S(1)}, f32[2048]{0:T(1024)S(1)}, f32[256]{0:T(256)S(1)}) all-reduce(f32[1024]{0:T(1024)S(1)} %bitcast.125, f32[1024]{0:T(1024)S(1)} %bitcast.126, f32[1024]{0:T(1024)S(1)} %bitcast.124, ...), channel_id=11, replica_groups=mesh['dp'=4,'seq'=8] {'dp','seq'}, use_global_device_ids=true, to_apply=%region_20.21.clone | all-reduce | flops 5376 | bytes 43008
  380.4 194.1 %all-reduce.20.cloned.1.call-done = (f32[131072]{0:T(1024)}, f32[786432]{0:T(1024)}, f32[262144]{0:T(1024)}, f32[1048576]{0:T(1024)}, f32[1048576]{0:T(1024)}) async-done(((f32[131072]{0:T(1024)}, f32[786432]{0:T(1024)}, f32[262144]{0:T(1024)}, f32[1048576]{0:T(1024)}, f32[1048576]{0:T(1024)}), (f32[131072]{0:T(1024)}, f32[786432]{0:T(1024)}, f32[262144]{0:T(1024)}, f32[1048576]{0:T(1024)}, ...) | async-done | bytes 13107216
  574.6 1.6 dynamic-slice.5
  576.1 1.6 dynamic-slice.6
  580.4 1.5 dynamic-slice.3
  (189 shorter events, 33.8 us)
Async XLA Ops:
  7.2 90.0 %all-gather.8.cloned.1.call-start = ((), (), s32[]{:S(2)}) async-start(), calls=%async_computation.2 | async-start | bytes 1622016 | tf_op jit(solution)/shard_map/all_gather | solution.py:179
  7.9 138.9 %all-gather.10.cloned.1.call-start = ((), (), s32[]{:S(2)}) async-start(), calls=%async_computation.3 | async-start | bytes 2162688 | tf_op jit(solution)/shard_map/all_gather | solution.py:181
  8.7 93.9 %copy-start.24 = (bf16[8192]{0:T(1024)(128)(2,1)S(1)}, bf16[8192]{0:T(1024)(128)(2,1)}, u32[]{:S(2)}) copy-start(bf16[8192]{0:T(1024)(128)(2,1)} %param.18) | copy-start | bytes 49156
  8.7 177.8 %all-gather.12.cloned.1.call-start = ((), (), s32[]{:S(2)}) async-start(), calls=%async_computation.4 | async-start | bytes 2162688 | tf_op jit(solution)/shard_map/all_gather | solution.py:182
  9.4 200.1 %all-gather.16.cloned.1.call-start = ((), (), s32[]{:S(2)}) async-start(), calls=%async_computation.8 | async-start | bytes 1179648 | tf_op jit(solution)/shard_map/all_gather | solution.py:202
  96.9 49.4 %copy-start.32 = (f32[128]{0:T(128)}, f32[128]{0:T(128)S(1)}, u32[]{:S(2)}) copy-start(f32[128]{0:T(128)S(1)} %broadcast_multiply_fusion.1) | copy-start | bytes 1540
  97.1 5.4 copy-start.45
  97.1 49.7 %copy-start.36 = (f32[128]{0:T(128)}, f32[128]{0:T(128)S(1)}, u32[]{:S(2)}) copy-start(f32[128]{0:T(128)S(1)} %fusion.51) | copy-start | bytes 1540
  97.1 142.8 %copy-start.27 = (f32[512]{0:T(512)}, f32[512]{0:T(512)S(1)}, u32[]{:S(2)}) copy-start(f32[512]{0:T(512)S(1)} %get-tuple-element.130) | copy-start | bytes 6148
  100.5 50.5 %copy-start.9 = (bf16[512,1536]{1,0:T(8,128)(2,1)}, bf16[512,1536]{1,0:T(8,128)(2,1)S(1)}, u32[]{:S(2)}) copy-start(bf16[512,1536]{1,0:T(8,128)(2,1)S(1)} %reshape.371) | copy-start | bytes 4718596
  101.7 131.6 %all-gather.14.cloned.1.call-start = ((), (), s32[]{:S(2)}) async-start(), calls=%async_computation.7 | async-start | bytes 1179648 | tf_op jit(solution)/shard_map/all_gather | solution.py:203
  102.3 186.0 %reduce-scatter.5.cloned.1.call-start = ((), (), s32[]{:S(2)}) async-start(), calls=%async_computation.6 | async-start | bytes 2359296 | tf_op jit(solution)/shard_map/reduce_scatter | solution.py:275
  189.6 54.2 %copy-start.4 = (bf16[2048,512]{1,0:T(8,128)(2,1)}, bf16[2048,512]{1,0:T(8,128)(2,1)S(1)}, u32[]{:S(2)}) copy-start(bf16[2048,512]{1,0:T(8,128)(2,1)S(1)} %reshape.380) | copy-start | bytes 6291460
  235.6 4.3 copy-start.6
  239.7 23.2 %copy-start.2 = (f32[128,512]{1,0:T(8,128)}, f32[128,512]{1,0:T(8,128)S(1)}, u32[]{:S(2)}) copy-start(f32[128,512]{1,0:T(8,128)S(1)} %get-tuple-element.121) | copy-start | bytes 786436
  239.7 7.1 %copy-start.34 = (f32[128]{0:T(128)}, f32[128]{0:T(128)S(1)}, u32[]{:S(2)}) copy-start(f32[128]{0:T(128)S(1)} %broadcast_multiply_fusion) | copy-start | bytes 1540
  239.9 6.9 %copy-start.38 = (f32[128]{0:T(128)}, f32[128]{0:T(128)S(1)}, u32[]{:S(2)}) copy-start(f32[128]{0:T(128)S(1)} %fusion.52) | copy-start | bytes 1540
  240.0 3.8 copy-start.20
  247.7 81.4 %copy-start.7 = (f32[128,512]{1,0:T(8,128)}, f32[128,512]{1,0:T(8,128)S(1)}, u32[]{:S(2)}) copy-start(f32[128,512]{1,0:T(8,128)S(1)} %get-tuple-element.97) | copy-start | bytes 786436
  248.1 4.7 copy-start.11
  252.7 72.3 %reduce-scatter.3.cloned.1.call-start = ((), (), s32[]{:S(2)}) async-start(), calls=%async_computation.5 | async-start | bytes 2359296 | tf_op jit(solution)/shard_map/reduce_scatter | solution.py:274
  258.2 4.6 copy-start.17
  260.0 314.5 %all-reduce.20.cloned.1.call-start = ((), (), s32[]{:S(2)}) async-start(), calls=%async_computation.9 | async-start | bytes 26214400
  267.3 58.8 %copy-start.33 = (f32[128]{0:T(128)S(1)}, f32[128]{0:T(128)}, u32[]{:S(2)}) copy-start(f32[128]{0:T(128)} %copy-done.32) | copy-start | bytes 1540
  267.3 58.8 %copy-start.37 = (f32[128]{0:T(128)S(1)}, f32[128]{0:T(128)}, u32[]{:S(2)}) copy-start(f32[128]{0:T(128)} %copy-done.36) | copy-start | bytes 1540
  270.4 58.4 %copy-start.46 = (f32[128]{0:T(128)S(1)}, f32[128]{0:T(128)}, u32[]{:S(2)}) copy-start(f32[128]{0:T(128)} %copy-done.45) | copy-start | bytes 1540
  270.4 58.7 %copy-start.40 = (s32[1,128]{1,0:T(1,128)S(1)}, s32[1,128]{1,0:T(1,128)}, u32[]{:S(2)}) copy-start(s32[1,128]{1,0:T(1,128)} %param.14) | copy-start | bytes 1540
  288.3 42.3 %copy-start.18 = (f32[1,128,512]{1,2,0:T(8,128)S(1)}, f32[1,128,512]{1,2,0:T(8,128)}, u32[]{:S(2)}) copy-start(f32[1,128,512]{1,2,0:T(8,128)} %reduce-scatter.5.cloned.1.call-done) | copy-start | bytes 786436
  325.0 5.6 copy-start.19
  334.0 45.7 %copy-start.8 = (f32[128,512]{1,0:T(8,128)S(1)}, f32[128,512]{1,0:T(8,128)}, u32[]{:S(2)}) copy-start(f32[128,512]{1,0:T(8,128)} %copy-done.7) | copy-start | bytes 786436
  334.0 45.7 %copy-start.13 = (f32[128,512]{1,0:T(8,128)S(1)}, f32[128,512]{1,0:T(8,128)}, u32[]{:S(2)}) copy-start(f32[128,512]{1,0:T(8,128)} %copy-done.12) | copy-start | bytes 786436
  334.0 45.6 %copy-start.42 = (f32[128]{0:T(128)S(1)}, f32[128]{0:T(128)}, u32[]{:S(2)}) copy-start(f32[128]{0:T(128)} %copy-done.41) | copy-start | bytes 1540
  (25 other events, 51.0 us)
Sparse Core Ops, SparseCore 0:
  11.0 58.0 all-gather.7
  72.1 55.5 all-gather.9
  130.7 55.7 all-gather.11
  188.5 20.9 all-gather.15
  211.5 21.7 all-gather.13
  252.8 35.3 reduce-scatter.4
  290.6 34.4 reduce-scatter.2
  334.2 240.3 all-reduce.19
where the time goes:
time: 590 us; the launch traced here: 589 us
  waiting for transfers between devices  321 us (54%)
  blocking collectives  165 us (28%)
  local copies, waits for them, and re-layouts  45.4 us (8%)
  matrix products  34.4 us (6%)
  between operations  14.8 us (3%)
  other arithmetic  7.45 us (1%)
    unnamed x9, waiting for transfers between devices  197 us
    unnamed x2, blocking collectives  77 us
    all_gather x1, blocking collectives, local(): lax.all_gather(owned[0], ('dp', 'seq'), axis=0, tiled=True)  44.7 us
    all_gather x1, blocking collectives, local(): lax.all_gather(owned[2], ('dp', 'seq'), axis=0, tiled=True)  43.2 us
    reduce_scatter x1, waiting for transfers between devices, local(): lax.psum_scatter(grad_keys, 'seq', scatter_dimension=1, tiled=True)  35.7 us
    all_gather x1, waiting for transfers between devices, local(): lax.all_gather(owned[4], ('dp', 'seq'), axis=0, tiled=True)  35.5 us
    unnamed x125, local copies, waits for them, and re-layouts  26.6 us
    all_gather x1, waiting for transfers between devices, local(): lax.all_gather(key_rows, 'seq', axis=1, tiled=True)  19.9 us
  transfers between devices with their start and end apart: 8, of which 6 were waited for; matrix products, arithmetic and copies ran while one was open for 8% of the time, Pallas kernels for 0%

commit v1 on v0

--- a/solution.py
+++ b/solution.py
@@ -1,6 +1,10 @@
+import types
+
 import jax
 import jax.numpy as jnp
 from jax import lax
+from jax.experimental import pallas as pl
+from jax.experimental.pallas import tpu as pltpu
 from jax.sharding import PartitionSpec as P
 
 D = 512
@@ -328,7 +332,717 @@
     )
 
 
+BF16 = jnp.bfloat16
+F32 = jnp.float32
+ROWS = 128
+PAIR = 128
+KEYS_AT = (0, 256, 768, 1536)
+ROOT_HALF = 0.7071067811865476
+ROOT_TAU = 0.3989422804014327
+
+
+def dot_nn(a, b):
+    return jnp.dot(a, b, preferred_element_type=F32)
+
+
+def dot_nt(a, b):
+    return lax.dot_general(a, b, (((1,), (1,)), ((), ())), preferred_element_type=F32)
+
+
+def dot_tn(a, b):
+    return lax.dot_general(a, b, (((0,), (0,)), ((), ())), preferred_element_type=F32)
+
+
+class Net:
+    def __init__(self, send_sems, recv_sems):
+        self.send_sems, self.recv_sems, self.copies = send_sems, recv_sems, []
+
+    def send(self, src, dst, device):
+        at = len(self.copies)
+        copy = pltpu.make_async_remote_copy(
+            src_ref=src,
+            dst_ref=dst,
+            send_sem=self.send_sems.at[at],
+            recv_sem=self.recv_sems.at[at],
+            device_id=device,
+            device_id_type=pl.DeviceIdType.MESH,
+        )
+        copy.start()
+        self.copies.append(copy)
+        return copy
+
+    def drain(self):
+        for copy in self.copies:
+            copy.wait_send()
+
+
+class Place:
+    def __init__(self):
+        dp, seq = lax.axis_index("dp"), lax.axis_index("seq")
+        self.dp, self.seq = dp, seq
+        self.y, self.x = lax.div(dp, 2), lax.rem(dp, 2)
+        self.z, self.c = lax.div(seq, 2), lax.rem(seq, 2)
+        self.flat = dp * 8 + seq
+
+    def dev(self, y, x, z, c):
+        return (y * 2 + x, z * 2 + c)
+
+    def sibling(self):
+        return self.dev(self.y, self.x, self.z, 1 - self.c)
+
+    def across_x(self):
+        return self.dev(self.y, 1 - self.x, self.z, self.c)
+
+    def across_y(self):
+        return self.dev(1 - self.y, self.x, self.z, self.c)
+
+    def ahead(self, step):
+        return lax.rem(self.z + step, 4)
+
+    def behind(self, step):
+        return lax.rem(self.z + (4 - step), 4)
+
+    def along_z(self, step):
+        return self.dev(self.y, self.x, self.ahead(step), self.c)
+
+
+class Gather:
+    def __init__(self, net, at, full, sources=None):
+        self.net, self.at, self.full, self.sources = net, at, full, sources
+
+    def along_z(self):
+        at = self.at
+        own = self.full.at[at.y, at.x, at.z, at.c]
+        self.waits = []
+        for step in (1, 2, 3):
+            src = own if self.sources is None else self.sources.at[at.ahead(step)]
+            self.waits.append(self.net.send(src, own, at.along_z(step)))
+
+    def arrive(self):
+        for copy in self.waits:
+            copy.wait_recv()
+
+    def first(self):
+        self.arrive()
+        at, full = self.at, self.full
+        low = full.at[at.y, at.x, 0:2, at.c]
+        high = full.at[at.y, at.x, 2:4, at.c]
+        self.waits = [
+            self.net.send(low, low, at.across_x()),
+            self.net.send(high, high, at.across_y()),
+        ]
+
+    def second(self):
+        self.arrive()
+        at, full = self.at, self.full
+        low = full.at[at.y, :, 0:2, at.c]
+        high = full.at[:, at.x, 2:4, at.c]
+        self.waits = [
+            self.net.send(low, low, at.across_y()),
+            self.net.send(high, high, at.across_x()),
+        ]
+
+    def cores(self):
+        self.arrive()
+        half = self.full.at[:, :, :, self.at.c]
+        self.waits = [self.net.send(half, half, self.at.sibling())]
+
+
+class Scatter:
+    def __init__(self, net, at, part, bufs):
+        self.net, self.at, self.part = net, at, part
+        self.sums, self.low1, self.high1, self.low2, self.high2, self.last = bufs
+
+    def arrive(self):
+        for copy in self.waits:
+            copy.wait_recv()
+
+    def cores(self):
+        at = self.at
+        self.waits = [self.net.send(self.part.at[:, :, :, 1 - at.c], self.sums, at.sibling())]
+
+    def first(self):
+        self.arrive()
+        at, sums, part = self.at, self.sums, self.part
+
+        def add(i, carry):
+            y, x, z = lax.div(i, 8), lax.rem(lax.div(i, 4), 2), lax.rem(i, 4)
+            sums[y, x, z] = sums[y, x, z] + part[y, x, z, at.c]
+            return carry
+
+        lax.fori_loop(0, 16, add, 0)
+        self.waits = [
+            self.net.send(sums.at[:, 1 - at.x, 0:2], self.low1, at.across_x()),
+            self.net.send(sums.at[1 - at.y, :, 2:4], self.high1, at.across_y()),
+        ]
+
+    def second(self):
+        self.arrive()
+        at, sums = self.at, self.sums
+
+        def add(i, carry):
+            a, b = lax.div(i, 2), lax.rem(i, 2)
+            sums[a, at.x, b] = sums[a, at.x, b] + self.low1[a, b]
+            sums[at.y, a, b + 2] = sums[at.y, a, b + 2] + self.high1[a, b]
+            return carry
+
+        lax.fori_loop(0, 4, add, 0)
+        self.waits = [
+            self.net.send(sums.at[1 - at.y, at.x, 0:2], self.low2, at.across_y()),
+            self.net.send(sums.at[at.y, 1 - at.x, 2:4], self.high2, at.across_x()),
+        ]
+
+    def along_z(self):
+        self.arrive()
+        at, sums = self.at, self.sums
+        for b in range(2):
+            sums[at.y, at.x, b] = sums[at.y, at.x, b] + self.low2[b]
+            sums[at.y, at.x, b + 2] = sums[at.y, at.x, b + 2] + self.high2[b]
+        self.waits = [
+            self.net.send(sums.at[at.y, at.x, at.ahead(s)], self.last.at[s - 1], at.along_z(s))
+            for s in (1, 2, 3)
+        ]
+
+    def total(self):
+        self.arrive()
+        at = self.at
+        total = self.sums[at.y, at.x, at.z].astype(F32)
+        for i in range(3):
+            total = total + self.last[i].astype(F32)
+        return total
+
+
+def spread(ref, value, width):
+    for j in range(width):
+        ref[pl.ds(j, value.shape[0], stride=width), :] = value[:, 128 * j : 128 * j + 128]
+
+
+def norm_parts(hidden):
+    centered = hidden - jnp.mean(hidden, axis=-1, keepdims=True)
+    spread_of = jnp.mean(centered * centered, axis=-1, keepdims=True)
+    inverse = lax.rsqrt(spread_of + EPSILON)
+    return centered * inverse, inverse
+
+
+def norm_back(upstream, gain_row, normal, inverse):
+    scaled = upstream * gain_row
+    return inverse * (
+        scaled
+        - jnp.mean(scaled, axis=-1, keepdims=True)
+        - normal * jnp.mean(scaled * normal, axis=-1, keepdims=True)
+    )
+
+
+def column_sum(value):
+    return jnp.sum(value, axis=0, keepdims=True)
+
+
+SHARDS = dict(emb=(32, 128), qkv=(16, 384), out=(16, 512), up=(16, 2048), down=(64, 512))
+
+
+def scratch():
+    vm = pltpu.VMEM
+    s = dict(
+        lin32=vm((256, 128), F32),
+        emb32=vm((1024, 128), F32),
+        qkv_src=vm((4, 16, 384), BF16),
+        small_w=vm((2, 2, 4, 2, 8, 128), F32),
+        small32=vm((256, 128), F32),
+        vecs=vm((16, 512), F32),
+        rel_row=vm((1, 256), F32),
+        bias_row=vm((1, 2048), F32),
+        picks=vm((256, 128), BF16),
+        start=vm((128, 512), F32),
+        normal1=vm((128, 512), F32),
+        inverse1=vm((128, 1), F32),
+        normed1=vm((4, 128, 512), BF16),
+        query=vm((4, 128, 128), BF16),
+        keyval=vm((2, 4, 2, 128, 128), BF16),
+        probs=vm((2, 128, 2560), F32),
+        mixed_out=vm((4, 128, 128), BF16),
+        mixed=vm((128, 512), BF16),
+        middle=vm((128, 512), F32),
+        normal2=vm((128, 512), F32),
+        inverse2=vm((128, 1), F32),
+        normed2=vm((128, 512), BF16),
+        acc1=vm((128, 512), F32),
+        acc2=vm((128, 512), F32),
+        gub=vm((1, 2048), F32),
+        grad_mid=vm((128, 512), F32),
+        gmix_src=vm((128, 512), BF16),
+        gmix=vm((4, 128, 128), BF16),
+        dkv=vm((2, 4, 2, 128, 128), F32),
+        dkv_in=vm((2, 4, 128, 128), F32),
+        dquery=vm((4, 128, 128), BF16),
+        dproj=vm((4, 128, 384), BF16),
+        gnorm=vm((4, 128, 512), BF16),
+        gnorm_in=vm((3, 128, 512), BF16),
+        sg=vm((16, 512), F32),
+        sg_in=vm((6, 16, 512), F32),
+        gathered=vm((4, 16, 384), BF16),
+        small_z=vm((3, 16, 512), F32),
+        sg_total=vm((16, 512), F32),
+    )
+    for name, shard in SHARDS.items():
+        s["w_" + name] = vm((2, 2, 4, 2) + shard, BF16)
+        s["g_" + name] = vm((2, 2, 4, 2) + shard, BF16)
+        s["r0_" + name] = vm((2, 2, 4) + shard, BF16)
+        s["r1_" + name] = vm((2, 2) + shard, BF16)
+        s["r2_" + name] = vm((2, 2) + shard, BF16)
+        s["r3_" + name] = vm((2,) + shard, BF16)
+        s["r4_" + name] = vm((2,) + shard, BF16)
+        s["r5_" + name] = vm((3,) + shard, BF16)
+    s["send_sems"] = pltpu.SemaphoreType.DMA((160,))
+    s["recv_sems"] = pltpu.SemaphoreType.DMA((160,))
+    return s
+
+
+INPUTS = ["stream", "ids", "cot", "emb", "qkv", "out", "up", "down", "small"]
+OUTPUTS = ["act", "gstream", "o_emb", "o_qkv", "o_out", "o_up", "o_down", "o_small"]
+
+
+def fused_kernel(*refs):
+    names = INPUTS + OUTPUTS + list(scratch())
+    v = types.SimpleNamespace(**dict(zip(names, refs, strict=True)))
+    at = Place()
+    net = Net(v.send_sems, v.recv_sems)
+    y, x, z, c = at.y, at.x, at.z, at.c
+
+    barrier = pltpu.get_barrier_semaphore()
+    peers = [at.sibling(), at.across_x(), at.across_y()] + [at.along_z(s) for s in (1, 2, 3)]
+    for peer in peers:
+        pl.semaphore_signal(
+            barrier, inc=1, device_id=peer, device_id_type=pl.DeviceIdType.MESH
+        )
+
+    v.w_emb[y, x, z, c] = v.emb[...]
+    v.small_w[y, x, z, c] = v.small[...]
+    v.lin32[0:192, :] = v.qkv[...].astype(F32)
+    for t in range(3):
+        for zz in range(4):
+            piece = v.lin32[pl.ds(4 * t + zz, 16, stride=12), :].astype(BF16)
+            v.qkv_src[zz, :, 128 * t : 128 * t + 128] = piece
+    v.w_qkv[y, x, z, c] = v.qkv_src[z]
+    v.lin32[0:64, :] = v.out[...].astype(F32)
+    for j in range(4):
+        v.w_out[y, x, z, c, :, 128 * j : 128 * j + 128] = v.lin32[
+            pl.ds(j, 16, stride=4), :
+        ].astype(BF16)
+    v.lin32[...] = v.up[...].astype(F32)
+    for j in range(16):
+        v.w_up[y, x, z, c, :, 128 * j : 128 * j + 128] = v.lin32[
+            pl.ds(j, 16, stride=16), :
+        ].astype(BF16)
+    v.lin32[...] = v.down[...].astype(F32)
+    for j in range(4):
+        v.w_down[y, x, z, c, :, 128 * j : 128 * j + 128] = v.lin32[
+            pl.ds(j, 64, stride=4), :
+        ].astype(BF16)
+    pl.semaphore_wait(barrier, len(peers))
+
+    emb = Gather(net, at, v.w_emb)
+    small = Gather(net, at, v.small_w)
+    qkv = Gather(net, at, v.w_qkv, v.qkv_src)
+    out = Gather(net, at, v.w_out)
+    up = Gather(net, at, v.w_up)
+    down = Gather(net, at, v.w_down)
+    fast, slow = (emb, small, qkv), (out, up, down)
+    for g in fast:
+        g.along_z()
+    for g in slow:
+        g.along_z()
+    for g in fast:
+        g.first()
+    for g in fast:
+        g.second()
+    v.picks[...] = (
+        (lax.broadcasted_iota(jnp.int32, (VOCAB, ROWS), 0) == v.ids[...]).astype(F32).astype(BF16)
+    )
+    for g in fast:
+        g.cores()
+    emb.arrive()
+    small.arrive()
+
+    v.small32[...] = v.small_w[...].reshape(256, 128)
+    lane = lax.broadcasted_iota(jnp.int32, (128, 512), 1)
+    row = lax.broadcasted_iota(jnp.int32, (128, 512), 0)
+    owner = lax.broadcasted_iota(jnp.int32, (32, 512), 0)
+    where = lax.broadcasted_iota(jnp.int32, (32, 512), 1)
+
+    def tiled(kind, size):
+        pieces = v.small32[pl.ds(kind, 32, stride=8), :].astype(BF16)
+        select = (lax.rem(lane, size) == row).astype(F32).astype(BF16)
+        return dot_nn(pieces, select)
+
+    def picked(wide, size, first):
+        return column_sum(jnp.where(owner == first + lax.div(where, size), wide, 0.0))
+
+    for kind in range(3):
+        wide = tiled(kind, 32)
+        for half in range(2):
+            v.vecs[2 * kind + half : 2 * kind + half + 1, :] = picked(wide, 32, 16 * half)
+    wide = tiled(3, 64)
+    for block in range(4):
+        v.bias_row[:, 512 * block : 512 * block + 512] = picked(wide, 64, 8 * block)
+    rel_row = picked(tiled(4, 8), 8, 0)[:, 0:256]
+    rel_lane = lax.broadcasted_iota(jnp.int32, (1, 256), 1)
+
+    v.emb32[...] = v.w_emb[...].reshape(1024, 128).astype(F32)
+    for j in range(4):
+        cut = slice(128 * j, 128 * j + 128)
+        table = v.emb32[pl.ds(j, VOCAB, stride=4), :].astype(BF16)
+        v.start[:, cut] = v.stream[:, cut].astype(F32) + dot_tn(v.picks[...], table)
+    normal, inverse = norm_parts(v.start[...])
+    v.normal1[...] = normal
+    v.inverse1[...] = inverse
+    v.normed1[z] = (normal * v.vecs[0:1, :] + v.vecs[2:3, :]).astype(BF16)
+    normed_moves = [None] + [
+        net.send(v.normed1.at[z], v.normed1.at[z], at.along_z(s)) for s in (1, 2, 3)
+    ]
+
+    for g in slow:
+        g.first()
+
+    qkv.arrive()
+    weight = v.w_qkv[...].reshape(512, 384)
+    moves = []
+    for s in range(4):
+        if s:
+            normed_moves[s].wait_recv()
+        zs = at.behind(s)
+        projected = dot_nn(v.normed1[zs], weight).astype(BF16)
+        v.query[zs] = projected[:, 0:128]
+        v.keyval[0, zs, c] = projected[:, 128:256]
+        v.keyval[1, zs, c] = projected[:, 256:384]
+        both = v.keyval.at[:, zs, c]
+        moves.append(net.send(both, both, at.sibling()))
+        if s == 1:
+            for g in slow:
+                g.second()
+    for copy in moves:
+        copy.wait_recv()
+
+    pair_lane = lax.broadcasted_iota(jnp.int32, (ROWS, PAIR), 1)
+    head_lanes = (pair_lane < HEAD_DIM, pair_lane >= HEAD_DIM)
+
+    def rel_value(head, distance):
+        spot = (2 * z + head) * BUCKETS + distance
+        return jnp.sum(jnp.where(rel_lane == spot, rel_row, 0.0), axis=1, keepdims=True)
+
+    rel_values = [[rel_value(h, d) for d in range(4)] for h in range(2)]
+    zero = jnp.zeros((), BF16)
+    for zq in range(4):
+        count = 256 * (zq + 1)
+        keys = v.keyval[0, 0 : zq + 1].reshape(count, PAIR)
+        vals = v.keyval[1, 0 : zq + 1].reshape(count, PAIR)
+        heads = []
+        for h in range(2):
+            query = jnp.where(head_lanes[h], v.query[zq], zero)
+            bias = jnp.concatenate(
+                [
+                    jnp.broadcast_to(rel_values[h][zq - zk], (1, 256))
+                    for zk in range(zq + 1)
+                ],
+                axis=1,
+            )
+            scores = dot_nt(query, keys) * SCALING + bias
+            shifted = jnp.exp(scores - jnp.max(scores, axis=-1, keepdims=True))
+            probs = shifted / jnp.sum(shifted, axis=-1, keepdims=True)
+            v.probs[h, :, KEYS_AT[zq] : KEYS_AT[zq] + count] = probs
+            heads.append(dot_nn(probs.astype(BF16), vals))
+        v.mixed_out[zq] = jnp.where(head_lanes[0], heads[0], heads[1]).astype(BF16)
+    own_lanes = pl.ds(pl.multiple_of(z * PAIR, PAIR), PAIR)
+    moves = [
+        net.send(v.mixed_out.at[at.ahead(s)], v.mixed.at[:, own_lanes], at.along_z(s))
+        for s in (1, 2, 3)
+    ]
+    v.mixed[:, own_lanes] = v.mixed_out[z]
+    for g in slow:
+        g.cores()
+    for copy in moves:
+        copy.wait_recv()
+
+    out.arrive()
+    mixed = v.mixed[...]
+    out_weight = v.w_out[...].reshape(512, 512)
+    middle = v.start[...] + dot_nn(mixed, out_weight) + v.vecs[4:5, :]
+    v.middle[...] = middle
+    normal, inverse = norm_parts(middle)
+    v.normal2[...] = normal
+    v.inverse2[...] = inverse
+    v.normed2[...] = (normal * v.vecs[1:2, :] + v.vecs[3:4, :]).astype(BF16)
+    v.acc1[...] = jnp.zeros_like(v.acc1)
+    v.acc2[...] = jnp.zeros_like(v.acc2)
+    up.arrive()
+    down.arrive()
+
+    def hidden_tile(i, carry):
+        cols = pl.ds(pl.multiple_of(i * 256, 256), 256)
+        ty, tx, tz = lax.div(i, 4), lax.rem(lax.div(i, 2), 2), lax.rem(i, 2) * 2
+        normed = v.normed2[...]
+        grad = v.cot[...]
+        up_tile = v.w_up[:, :, :, :, :, cols].reshape(512, 256)
+        down_tile = v.w_down[ty, tx, pl.ds(tz, 2)].reshape(256, 512)
+        lifted = dot_nn(normed, up_tile) + v.bias_row[:, cols]
+        share = 0.5 * (1.0 + lax.erf(lifted * ROOT_HALF))
+        active = (lifted * share).astype(BF16)
+        slope = share + lifted * (jnp.exp(-0.5 * lifted * lifted) * ROOT_TAU)
+        v.acc1[...] += dot_nn(active, down_tile)
+        grad_lifted = dot_nt(grad, down_tile) * slope
+        v.gub[:, cols] = column_sum(grad_lifted)
+        low = grad_lifted.astype(BF16)
+        v.acc2[...] += dot_nt(low, up_tile)
+        v.g_down[ty, tx, pl.ds(tz, 2)] = dot_tn(active, grad).astype(BF16).reshape(2, 2, 64, 512)
+        v.g_up[:, :, :, :, :, cols] = dot_tn(normed, low).astype(BF16).reshape(2, 2, 4, 2, 16, 256)
+        return carry
+
+    lax.fori_loop(0, 8, hidden_tile, 0)
+
+    def scatter(name):
+        bufs = [getattr(v, f"r{i}_{name}") for i in range(6)]
+        return Scatter(net, at, getattr(v, "g_" + name), bufs)
+
+    s_down, s_up, s_out, s_qkv, s_emb = (
+        scatter(n) for n in ("down", "up", "out", "qkv", "emb")
+    )
+    s_down.cores()
+    s_up.cores()
+    grad_wide = v.cot[...].astype(F32)
+    v.act[...] = (v.middle[...] + v.acc1[...] + v.vecs[5:6, :]).astype(BF16)
+    upstream = v.acc2[...]
+    normal = v.normal2[...]
+    v.sg[1:2, :] = column_sum(upstream * normal)
+    v.sg[3:4, :] = column_sum(upstream)
+    v.sg[5:6, :] = column_sum(grad_wide)
+    grad_middle = grad_wide + norm_back(upstream, v.vecs[1:2, :], normal, v.inverse2[...])
+    v.grad_mid[...] = grad_middle
+    v.sg[4:5, :] = column_sum(grad_middle)
+    for block in range(4):
+        v.sg[6 + block : 7 + block, :] = v.gub[:, 512 * block : 512 * block + 512]
+    middle_low = grad_middle.astype(BF16)
+    v.gmix_src[...] = dot_nt(middle_low, v.w_out[...].reshape(512, 512)).astype(BF16)
+    moves = [
+        net.send(
+            v.gmix_src.at[:, pl.ds(pl.multiple_of(at.ahead(s) * PAIR, PAIR), PAIR)],
+            v.gmix.at[z],
+            at.along_z(s),
+        )
+        for s in (1, 2, 3)
+    ]
+    v.gmix[z] = v.gmix_src[:, own_lanes]
+    v.g_out[...] = dot_tn(v.mixed[...], middle_low).astype(BF16).reshape(2, 2, 4, 2, 16, 512)
+    s_out.cores()
+    s_down.first()
+    s_up.first()
+    s_out.first()
+    for copy in moves:
+        copy.wait_recv()
+
+    rel_sums = [[jnp.zeros((1, 256), F32) for d in range(4)] for h in range(2)]
+    core_moves = {}
+    for zq in (3, 2, 1, 0):
+        count = 256 * (zq + 1)
+        keys = v.keyval[0, 0 : zq + 1].reshape(count, PAIR)
+        vals = v.keyval[1, 0 : zq + 1].reshape(count, PAIR)
+        heads, dkeys, dvals = [], 0.0, 0.0
+        for h in range(2):
+            query = jnp.where(head_lanes[h], v.query[zq], zero)
+            grad = jnp.where(head_lanes[h], v.gmix[zq], zero)
+            probs = v.probs[h, :, KEYS_AT[zq] : KEYS_AT[zq] + count]
+            grad_probs = dot_nt(grad, vals)
+            inner = jnp.sum(probs * grad_probs, axis=-1, keepdims=True)
+            grad_scores = probs * (grad_probs - inner)
+            for zk in range(zq + 1):
+                tile = grad_scores[:, 256 * zk : 256 * zk + 256]
+                rel_sums[h][zq - zk] = rel_sums[h][zq - zk] + column_sum(tile)
+            low = grad_scores.astype(BF16)
+            heads.append(dot_nn(low, keys))
+            dkeys = dkeys + dot_tn(low, query)
+            dvals = dvals + dot_tn(probs.astype(BF16), grad)
+        v.dquery[zq] = (jnp.where(head_lanes[0], heads[0], heads[1]) * SCALING).astype(BF16)
+        dkeys = dkeys.reshape(zq + 1, 2, ROWS, PAIR)
+        dvals = dvals.reshape(zq + 1, 2, ROWS, PAIR)
+        if zq == 3:
+            v.dkv[0] = dkeys
+            v.dkv[1] = dvals
+        else:
+            v.dkv[0, 0 : zq + 1] += dkeys
+            v.dkv[1, 0 : zq + 1] += dvals
+        core_moves[zq] = net.send(
+            v.dkv.at[:, zq, 1 - c], v.dkv_in.at[:, zq], at.sibling()
+        )
+        if zq == 2:
+            s_down.second()
+            s_up.second()
+            s_out.second()
+    weight = v.w_qkv[...].reshape(512, 384)
+    for zq in (3, 2, 1, 0):
+        core_moves[zq].wait_recv()
+        dkeys = (v.dkv[0, zq, c] + v.dkv_in[0, zq]) * SCALING
+        dvals = v.dkv[1, zq, c] + v.dkv_in[1, zq]
+        v.dproj[zq, :, 0:128] = v.dquery[zq]
+        v.dproj[zq, :, 128:256] = dkeys.astype(BF16)
+        v.dproj[zq, :, 256:384] = dvals.astype(BF16)
+        v.gnorm[zq] = dot_nt(v.dproj[zq], weight).astype(BF16)
+    gnorm_moves = [
+        net.send(v.gnorm.at[at.ahead(s)], v.gnorm_in.at[s - 1], at.along_z(s)) for s in (1, 2, 3)
+    ]
+    v.g_qkv[...] = (
+        dot_tn(v.normed1[...].reshape(512, 512), v.dproj[...].reshape(512, 384))
+        .astype(BF16)
+        .reshape(2, 2, 4, 2, 16, 384)
+    )
+    s_qkv.cores()
+    s_down.along_z()
+    s_up.along_z()
+    s_out.along_z()
+    s_qkv.first()
+    sums = jnp.zeros((1, 512), F32)
+    wide_lane = lax.broadcasted_iota(jnp.int32, (1, 512), 1)
+    for h in range(2):
+        for d in range(4):
+            spot = (2 * z + h) * BUCKETS + d
+            value = jnp.sum(rel_sums[h][d], axis=1, keepdims=True)
+            sums = sums + jnp.where(wide_lane == spot, value, 0.0)
+    v.sg[10:11, :] = sums
+    v.sg[11:16, :] = jnp.zeros((5, 512), F32)
+
+    upstream = v.gnorm[z].astype(F32)
+    for s in range(3):
+        gnorm_moves[s].wait_recv()
+        upstream = upstream + v.gnorm_in[s].astype(F32)
+    normal = v.normal1[...]
+    v.sg[0:1, :] = column_sum(upstream * normal)
+    v.sg[2:3, :] = column_sum(upstream)
+    grad_start = v.grad_mid[...] + norm_back(upstream, v.vecs[0:1, :], normal, v.inverse1[...])
+    start_low = grad_start.astype(BF16)
+    small_move = net.send(v.sg, v.sg_in.at[0], at.sibling())
+    grad_embed = dot_nn(v.picks[...], start_low)
+    spread(v.emb32, grad_embed, 4)
+    v.g_emb[...] = v.emb32[...].astype(BF16).reshape(2, 2, 4, 2, 32, 128)
+    s_emb.cores()
+    v.gstream[...] = start_low
+    s_qkv.second()
+    small_move.wait_recv()
+    v.sg_in[4] = v.sg[...] + v.sg_in[0]
+    small_move = net.send(v.sg_in.at[4], v.sg_in.at[1], at.across_x())
+    s_emb.first()
+    spread(v.o_down, s_down.total(), 4)
+    small_move.wait_recv()
+    v.sg_in[5] = v.sg_in[4] + v.sg_in[1]
+    small_move = net.send(v.sg_in.at[5], v.sg_in.at[2], at.across_y())
+    s_qkv.along_z()
+    s_emb.second()
+    spread(v.o_up, s_up.total(), 16)
+    small_move.wait_recv()
+    total = v.sg_in[5] + v.sg_in[2]
+    v.sg_in[3] = total
+    small_moves = [
+        net.send(v.sg_in.at[3], v.small_z.at[s - 1], at.along_z(s)) for s in (1, 2, 3)
+    ]
+    s_emb.along_z()
+    spread(v.o_out, s_out.total(), 4)
+    s_qkv.arrive()
+    v.gathered[z] = v.r0_qkv[y, x, z]
+    for s in (1, 2, 3):
+        v.gathered[at.behind(s)] = v.r5_qkv[s - 1]
+    for zz in range(4):
+        piece = v.gathered[zz].astype(F32)
+        for t in range(3):
+            v.o_qkv[pl.ds(4 * t + zz, 16, stride=12), :] = piece[:, 128 * t : 128 * t + 128]
+    for s in range(3):
+        small_moves[s].wait_recv()
+        total = total + v.small_z[s]
+    v.sg_total[...] = total
+
+    def shard(row_at, offset):
+        line = jnp.broadcast_to(v.sg_total[pl.ds(row_at, 1), :], (8, 512))
+        return pltpu.roll(line, lax.rem(512 - offset, 512), 1)[0:1, 0:128]
+
+    line = 32 * lax.rem(at.flat, 16)
+    v.o_small[0:1, :] = shard(y, line)
+    v.o_small[1:2, :] = shard(2 + y, line)
+    v.o_small[2:3, :] = shard(4 + y, line)
+    v.o_small[3:4, :] = shard(6 + at.dp, 64 * at.seq)
+    v.o_small[4:5, :] = shard(10, 8 * at.flat)
+    v.o_small[5:8, :] = jnp.zeros((3, 128), F32)
+    v.o_emb[...] = s_emb.total()
+    net.drain()
+
+
+def fused_local(
+    stream,
+    byte_ids,
+    cotangent,
+    embed_flat,
+    qkv_flat,
+    out_flat,
+    up_flat,
+    down_flat,
+    gains,
+    norm_shifts,
+    out_shifts,
+    up_bias,
+    rel_bias,
+):
+    def line(piece):
+        return jnp.pad(piece.astype(F32), (0, 128 - piece.shape[0]))[None]
+
+    small = jnp.concatenate(
+        [line(p) for p in (gains, norm_shifts, out_shifts, up_bias, rel_bias)]
+        + [jnp.zeros((3, 128), F32)]
+    )
+    operands = (
+        stream.reshape(ROWS, D),
+        byte_ids,
+        cotangent.reshape(ROWS, D),
+        embed_flat.reshape(-1, 128),
+        qkv_flat.reshape(-1, 128),
+        out_flat.reshape(-1, 128),
+        up_flat.reshape(-1, 128),
+        down_flat.reshape(-1, 128),
+        small,
+    )
+    shapes = (
+        ((ROWS, D), BF16),
+        ((ROWS, D), BF16),
+        ((32, 128), F32),
+        ((192, 128), F32),
+        ((64, 128), F32),
+        ((256, 128), F32),
+        ((256, 128), F32),
+        ((8, 128), F32),
+    )
+    whole = pl.BlockSpec(memory_space=pltpu.VMEM)
+    act, gstream, g_emb, g_qkv, g_out, g_up, g_down, g_small = pl.pallas_call(
+        fused_kernel,
+        out_shape=[jax.ShapeDtypeStruct(s, t) for s, t in shapes],
+        in_specs=[whole] * len(operands),
+        out_specs=[whole] * len(shapes),
+        scratch_shapes=list(scratch().values()),
+        compiler_params=pltpu.CompilerParams(
+            collective_id=0, has_side_effects=True, vmem_limit_bytes=60 << 20
+        ),
+        name="layer",
+    )(*operands)
+    return (
+        act.reshape(stream.shape),
+        gstream.reshape(stream.shape),
+        g_emb.reshape(-1),
+        g_qkv.reshape(-1),
+        g_out.reshape(-1),
+        g_up.reshape(-1),
+        g_down.reshape(-1),
+        g_small[0, : gains.shape[0]],
+        g_small[1, : norm_shifts.shape[0]],
+        g_small[2, : out_shifts.shape[0]],
+        g_small[3, : up_bias.shape[0]],
+        g_small[4, : rel_bias.shape[0]],
+    )
+
+
 def solution(mesh):
+    body = fused_local if (mesh.shape["dp"], mesh.shape["seq"]) == (4, 8) else local
     in_specs = (
         P("dp", "seq", None),
         P("dp", "seq"),
@@ -358,4 +1072,4 @@
         P(("dp", "seq")),
         P(("dp", "seq")),
     )
-    return jax.shard_map(local, mesh=mesh, in_specs=in_specs, out_specs=out_specs, check_vma=False)
+    return jax.shard_map(body, mesh=mesh, in_specs=in_specs, out_specs=out_specs, check_vma=False)

time: 590 us -> 124 us (0.21)
  waiting for transfers between devices: 321 us -> 0 us
  blocking collectives: 165 us -> 0 us
  Pallas kernels: 0 us -> 110 us
  matrix products: 34.4 us -> 0 us
  local copies, waits for them, and re-layouts: 45.4 us -> 11.6 us
  between operations: 14.8 us -> 0.67 us
  other arithmetic: 7.45 us -> 0.68 us
    unnamed x9 -> x0, waiting for transfers between devices: 197 us -> none
    pallas_call x0 -> x1, Pallas kernels: none -> 110 us  [fused_local(): pl.pallas_call(fused_kernel, out_shape=[jax.ShapeDtypeStruct(s, t) for s,...]
    all_gather x2 -> x0, blocking collectives: 87.9 us -> none  [the longest x1 44.7 us: local(): lax.all_gather(owned[0], ('dp', 'seq'), axis=0, tiled=True)]
    unnamed x2 -> x0, blocking collectives: 77 us -> none
    all_gather x5 -> x0, waiting for transfers between devices: 71.7 us -> none  [the longest x1 35.5 us: local(): lax.all_gather(owned[4], ('dp', 'seq'), axis=0, tiled=True)]
    reduce_scatter x2 -> x0, waiting for transfers between devices: 52.7 us -> none  [the longest x1 35.7 us: local(): lax.psum_scatter(grad_keys, 'seq', scatter_dimension=1, tiled=True)]
    dot_general x22 -> x0, matrix products: 34.4 us -> none  [the longest x1 4.58 us: row_back(): jnp.einsum('hqk,qhd->khd', soft_weights.astype(jnp.bfloat16), grad_heads,...]
    unnamed x125 -> x25, local copies, waits for them, and re-layouts: 26.6 us -> 7.25 us
  transfers between devices with their start and end apart: 8 -> 0, of which waited for: 6 -> 0; matrix products, arithmetic and copies ran while one was open for 8% -> 0% of each run, Pallas kernels for 0% -> 0%
where the time goes in v1:
time: 124 us; the launch traced here: 123 us
  Pallas kernels  110 us (89%)
  local copies, waits for them, and re-layouts  11.6 us (9%)
    pallas_call x1, Pallas kernels, fused_local(): pl.pallas_call(fused_kernel, out_shape=[jax.ShapeDtypeStruct(s, t) for s,...  110 us
    unnamed x25, local copies, waits for them, and re-layouts  7.25 us

profile of v1, /device:TPU:0, one launch (start us, length us, event | category | flops | bytes accessed | tf_op | source)
XLA Modules:
  0.0 123.3 jit_solution(18139614057428214413)
XLA Ops:
  0.6 0.7 bitcast_convert_fusion
  1.3 0.0 copy-start.6
  1.3 0.0 copy-start.7
  1.3 0.7 copy-done.6
  2.0 0.0 copy-done.7
  2.0 0.0 copy-start.8
  2.0 0.7 copy-done.8
  2.7 0.6 concatenate.3.refs_8_
  3.3 110.4 %layer.1 = (bf16[128,512]{1,0:T(8,128)(2,1)}, bf16[128,512]{1,0:T(8,128)(2,1)}, f32[32,128]{1,0:T(8,128)}, f32[192,128]{1,0:T(8,128)}, f32[64,128]{1,0:T(8,128)}...) custom-call(bf16[128,512]{1,0:T(8,128)(2,1)} %bitcast.39, s32[1,128]{1,0:T(1,128)} %refs_1_.1, ...), custom_call_target="tpu_custom_call" | custom-call | tf_op jit(solution)/shard_map/layer/pallas_call | solution.py:1017
  113.7 1.3 %slice_bitcast_fusion.2 = (f32[32]{0:T(128)}, f32[32]{0:T(128)}, f32[32]{0:T(128)}) fusion(f32[8,128]{1,0:T(8,128)} %get-tuple-element.27), kind=kLoop, calls=%fused_computation.7 | loop fusion | bytes 768 | tf_op jit(solution)/shard_map/squeeze | solution.py:1038
  115.0 1.2 slice_bitcast_fusion
  116.2 1.2 slice_bitcast_fusion.1
  117.4 0.0 copy-start.2
  117.4 1.6 %copy.32 = bf16[1,128,512]{2,1,0:T(8,128)(2,1)} copy(bf16[1,128,512]{2,1,0:T(8,128)(2,1)} %bitcast.44) | data formatting | bytes 262144
  119.0 0.0 copy-done.2
  119.0 0.0 copy-start.5
  119.0 0.0 copy-start.3
  119.0 0.7 copy.33
  119.7 0.1 copy-done.5
  119.7 0.6 copy.34
  120.3 0.0 copy-done.3
  120.4 0.0 copy-start.4
  120.4 0.0 copy-start.1
  120.4 0.6 copy.35
  121.0 0.1 copy-done.4
  121.1 0.6 copy.36
  121.7 0.0 copy-done.1
  121.7 0.0 copy-start
  121.7 0.7 copy.37
  122.4 0.3 copy-done
  122.7 0.7 copy.38
  (3 shorter events, 0.0 us)
Async XLA Ops:
  1.3 0.7 copy-start.6
  1.3 0.7 copy-start.7
  2.0 0.7 copy-start.8
  117.4 1.6 %copy-start.2 = (bf16[128,512]{1,0:T(8,128)(2,1)S(1)}, bf16[128,512]{1,0:T(8,128)(2,1)}, u32[]{:S(2)}) copy-start(bf16[128,512]{1,0:T(8,128)(2,1)} %get-tuple-element.21) | copy-start | bytes 393220
  119.0 0.7 copy-start.5
  119.0 1.3 %copy-start.3 = (f32[192,128]{1,0:T(8,128)S(1)}, f32[192,128]{1,0:T(8,128)}, u32[]{:S(2)}) copy-start(f32[192,128]{1,0:T(8,128)} %get-tuple-element.23) | copy-start | bytes 294916
  120.4 0.8 copy-start.4
  120.4 1.4 %copy-start.1 = (f32[256,128]{1,0:T(8,128)S(1)}, f32[256,128]{1,0:T(8,128)}, u32[]{:S(2)}) copy-start(f32[256,128]{1,0:T(8,128)} %get-tuple-element.25) | copy-start | bytes 393220
  121.7 1.0 copy-start

commit v2 on v1

--- a/solution.py
+++ b/solution.py
@@ -371,9 +371,25 @@
         self.copies.append(copy)
         return copy
 
+    def slots(self, count):
+        first = len(self.copies)
+        self.copies.extend([None] * count)
+        return first
+
+    def copy(self, src, dst, device, send_at, recv_at):
+        return pltpu.make_async_remote_copy(
+            src_ref=src,
+            dst_ref=dst,
+            send_sem=self.send_sems.at[send_at],
+            recv_sem=self.recv_sems.at[recv_at],
+            device_id=device,
+            device_id_type=pl.DeviceIdType.MESH,
+        )
+
     def drain(self):
         for copy in self.copies:
-            copy.wait_send()
+            if copy is not None:
+                copy.wait_send()
 
 
 class Place:
@@ -395,6 +411,22 @@
 
     def across_y(self):
         return self.dev(1 - self.y, self.x, self.z, self.c)
+
+    def near(self):
+        return self.z + 1 - 2 * lax.rem(self.z, 2)
+
+    def toward(self, z):
+        return self.dev(self.y, self.x, z, self.c)
+
+    def others(self):
+        return [
+            (dy, dx, dz) for dz in (2, 1, 3, 0) for dy in (1, 0) for dx in (1, 0) if dy + dx + dz
+        ]
+
+    def other(self, dy, dx, dz):
+        y = 1 - self.y if dy else self.y
+        x = 1 - self.x if dx else self.x
+        return y, x, self.ahead(dz)
 
     def ahead(self, step):
         return lax.rem(self.z + step, 4)
@@ -448,6 +480,110 @@
         self.waits = [self.net.send(half, half, self.at.sibling())]
 
 
+class Direct:
+    def __init__(self, net, at, full):
+        self.net, self.at, self.full = net, at, full
+
+    def start(self):
+        at = self.at
+        own = self.full.at[at.y, at.x, at.z, at.c]
+        self.waits = [
+            self.net.send(own, own, at.dev(*at.other(*way), at.c)) for way in at.others()
+        ]
+
+    def arrive(self):
+        for copy in self.waits:
+            copy.wait_recv()
+
+    def cores(self):
+        self.arrive()
+        half = self.full.at[:, :, :, self.at.c]
+        self.waits = [self.net.send(half, half, self.at.sibling())]
+
+
+class Owners:
+    def __init__(self, net, at, source, target):
+        self.net, self.at, self.source, self.target = net, at, source, target
+        self.first = net.slots(4)
+
+    def copy(self, k, sender):
+        first = self.first
+        return self.net.copy(
+            self.source(k), self.target(k), self.at.toward(k), first + k, first + sender
+        )
+
+    def send(self, k):
+        @pl.when(self.at.z != k)
+        def _():
+            self.copy(k, self.at.z).start()
+
+    def arrive(self):
+        for step in (1, 2, 3):
+            sender = self.at.ahead(step)
+            self.copy(sender, sender).wait_recv()
+
+    def drain(self):
+        for step in (1, 2, 3):
+            self.copy(self.at.ahead(step), self.at.z).wait_send()
+
+
+class Relayed:
+    def __init__(self, net, at, full):
+        self.net, self.at, self.full = net, at, full
+        far = at.ahead(2)
+        near = at.near()
+        self.zs = (at.z, near, far, lax.rem(near + 2, 4))
+        self.firsts, self.seconds, self.core_moves = [None] * 4, [None] * 4, [None] * 4
+
+    def block(self, z):
+        at = self.at
+        return self.full.at[at.y, at.x, z, at.c]
+
+    def first(self, k):
+        at = self.at
+        block = self.block(self.zs[k])
+        self.firsts[k] = self.net.send(block, block, at.across_y() if k % 2 else at.across_x())
+
+    def start(self):
+        at = self.at
+        own = self.block(at.z)
+        self.far = self.net.send(own, own, at.toward(self.zs[2]))
+        self.near = self.net.send(own, own, at.toward(self.zs[1]))
+        self.first(0)
+
+    def take_near(self):
+        self.near.wait_recv()
+        self.first(1)
+
+    def take_far(self):
+        self.far.wait_recv()
+        block = self.block(self.zs[2])
+        self.relay = self.net.send(block, block, self.at.toward(self.zs[1]))
+        self.first(2)
+
+    def take_relay(self):
+        self.relay.wait_recv()
+        self.first(3)
+
+    def second(self, k):
+        self.firsts[k].wait_recv()
+        at, z = self.at, self.zs[k]
+        if k % 2:
+            blocks, peer = self.full.at[:, at.x, z, at.c], at.across_x()
+        else:
+            blocks, peer = self.full.at[at.y, :, z, at.c], at.across_y()
+        self.seconds[k] = self.net.send(blocks, blocks, peer)
+
+    def cores(self, k):
+        self.seconds[k].wait_recv()
+        blocks = self.full.at[:, :, self.zs[k], self.at.c]
+        self.core_moves[k] = self.net.send(blocks, blocks, self.at.sibling())
+
+    def done(self):
+        for copy in self.core_moves:
+            copy.wait_recv()
+
+
 class Scatter:
     def __init__(self, net, at, part, bufs):
         self.net, self.at, self.part = net, at, part
@@ -492,23 +628,72 @@
             self.net.send(sums.at[at.y, 1 - at.x, 2:4], self.high2, at.across_x()),
         ]
 
-    def along_z(self):
+    def gathered(self):
         self.arrive()
         at, sums = self.at, self.sums
         for b in range(2):
             sums[at.y, at.x, b] = sums[at.y, at.x, b] + self.low2[b]
             sums[at.y, at.x, b + 2] = sums[at.y, at.x, b + 2] + self.high2[b]
+
+    def along_z(self):
+        self.gathered()
+        at, sums = self.at, self.sums
         self.waits = [
             self.net.send(sums.at[at.y, at.x, at.ahead(s)], self.last.at[s - 1], at.along_z(s))
             for s in (1, 2, 3)
         ]
 
+    def pair(self):
+        self.gathered()
+        at, sums, last = self.at, self.sums, self.last
+        near = at.near()
+        peer = at.toward(near)
+        beyond = sums.at[at.y, at.x, lax.rem(near + 2, 4)]
+        self.waits = [self.net.send(beyond, last.at[1], peer)]
+        self.near = self.net.send(sums.at[at.y, at.x, near], last.at[0], peer)
+
+    def far(self):
+        self.arrive()
+        at, sums, last = self.at, self.sums, self.last
+        far = at.ahead(2)
+        sums[at.y, at.x, far] = sums[at.y, at.x, far] + last[1]
+        self.waits = [
+            self.near,
+            self.net.send(sums.at[at.y, at.x, far], last.at[2], at.toward(far)),
+        ]
+
     def total(self):
         self.arrive()
         at = self.at
         total = self.sums[at.y, at.x, at.z].astype(F32)
-        for i in range(3):
-            total = total + self.last[i].astype(F32)
+        return total + self.last[0].astype(F32) + self.last[2].astype(F32)
+
+
+class DirectScatter:
+    def __init__(self, net, at, part, sums, landed):
+        self.net, self.at, self.part, self.sums, self.landed = net, at, part, sums, landed
+
+    def cores(self):
+        at = self.at
+        self.move = self.net.send(self.part.at[:, :, :, 1 - at.c], self.sums, at.sibling())
+
+    def start(self):
+        self.move.wait_recv()
+        at, sums = self.at, self.sums
+        sums[...] = sums[...] + self.part[:, :, :, at.c]
+        self.waits = []
+        for i, way in enumerate(at.others()):
+            y, x, z = at.other(*way)
+            self.waits.append(
+                self.net.send(sums.at[y, x, z], self.landed.at[i], at.dev(y, x, z, at.c))
+            )
+
+    def total(self):
+        at = self.at
+        total = self.sums[at.y, at.x, at.z].astype(F32)
+        for i, copy in enumerate(self.waits):
+            copy.wait_recv()
+            total = total + self.landed[i].astype(F32)
         return total
 
 
@@ -537,7 +722,25 @@
     return jnp.sum(value, axis=0, keepdims=True)
 
 
-SHARDS = dict(emb=(32, 128), qkv=(16, 384), out=(16, 512), up=(16, 2048), down=(64, 512))
+SHARDS = dict(emb=(48, 128), qkv=(16, 384), out=(16, 512), up=(16, 2048), down=(64, 512))
+
+
+INPUTS = [
+    "stream",
+    "ids",
+    "cot",
+    "emb",
+    "qkv",
+    "out",
+    "up",
+    "down",
+    "gains",
+    "shifts",
+    "outs",
+    "ubias",
+    "rel",
+]
+OUTPUTS = ["act", "gstream", "o_emb", "o_qkv", "o_out", "o_up", "o_down", "o_small"]
 
 
 def scratch():
@@ -546,8 +749,9 @@
         lin32=vm((256, 128), F32),
         emb32=vm((1024, 128), F32),
         qkv_src=vm((4, 16, 384), BF16),
-        small_w=vm((2, 2, 4, 2, 8, 128), F32),
-        small32=vm((256, 128), F32),
+        small32=vm((512, 128), F32),
+        select=vm((3, 128, 512), BF16),
+        landed=vm((15, 48, 128), BF16),
         vecs=vm((16, 512), F32),
         rel_row=vm((1, 256), F32),
         bias_row=vm((1, 2048), F32),
@@ -573,15 +777,12 @@
         gmix=vm((4, 128, 128), BF16),
         dkv=vm((2, 4, 2, 128, 128), F32),
         dkv_in=vm((2, 4, 128, 128), F32),
-        dquery=vm((4, 128, 128), BF16),
+        slope=vm((128, 2048), F32),
         dproj=vm((4, 128, 384), BF16),
         gnorm=vm((4, 128, 512), BF16),
-        gnorm_in=vm((3, 128, 512), BF16),
+        gnorm_in=vm((4, 128, 512), BF16),
         sg=vm((16, 512), F32),
-        sg_in=vm((6, 16, 512), F32),
         gathered=vm((4, 16, 384), BF16),
-        small_z=vm((3, 16, 512), F32),
-        sg_total=vm((16, 512), F32),
     )
     for name, shard in SHARDS.items():
         s["w_" + name] = vm((2, 2, 4, 2) + shard, BF16)
@@ -592,102 +793,115 @@
         s["r3_" + name] = vm((2,) + shard, BF16)
         s["r4_" + name] = vm((2,) + shard, BF16)
         s["r5_" + name] = vm((3,) + shard, BF16)
-    s["send_sems"] = pltpu.SemaphoreType.DMA((160,))
-    s["recv_sems"] = pltpu.SemaphoreType.DMA((160,))
+    for name, shape, kind in (
+        ("stream", (ROWS, D), BF16),
+        ("ids", (1, ROWS), jnp.int32),
+        ("cot", (ROWS, D), BF16),
+        ("emb", (32, 128), BF16),
+        ("qkv", (192, 128), BF16),
+        ("out", (64, 128), BF16),
+        ("up", (256, 128), BF16),
+        ("down", (256, 128), BF16),
+        ("gains", (1, 32), BF16),
+        ("shifts", (1, 32), BF16),
+        ("outs", (1, 32), BF16),
+        ("ubias", (1, 64), BF16),
+        ("rel", (1, 8), BF16),
+    ):
+        s[name] = vm(shape, kind)
+    s["in_sems"] = pltpu.SemaphoreType.DMA((len(INPUTS),))
+    s["send_sems"] = pltpu.SemaphoreType.DMA((240,))
+    s["recv_sems"] = pltpu.SemaphoreType.DMA((240,))
     return s
 
 
-INPUTS = ["stream", "ids", "cot", "emb", "qkv", "out", "up", "down", "small"]
-OUTPUTS = ["act", "gstream", "o_emb", "o_qkv", "o_out", "o_up", "o_down", "o_small"]
-
-
 def fused_kernel(*refs):
-    names = INPUTS + OUTPUTS + list(scratch())
+    hbm = ["h_" + name for name in INPUTS]
+    names = hbm + OUTPUTS + list(scratch())
     v = types.SimpleNamespace(**dict(zip(names, refs, strict=True)))
     at = Place()
     net = Net(v.send_sems, v.recv_sems)
     y, x, z, c = at.y, at.x, at.z, at.c
 
+    loads = {}
+    for i, name in enumerate(INPUTS):
+        loads[name] = pltpu.make_async_copy(
+            getattr(v, "h_" + name), getattr(v, name), v.in_sems.at[i]
+        )
+        loads[name].start()
     barrier = pltpu.get_barrier_semaphore()
-    peers = [at.sibling(), at.across_x(), at.across_y()] + [at.along_z(s) for s in (1, 2, 3)]
+    peers = [at.dev(*at.other(*way), c) for way in at.others()] + [at.sibling()]
     for peer in peers:
         pl.semaphore_signal(
             barrier, inc=1, device_id=peer, device_id_type=pl.DeviceIdType.MESH
         )
 
-    v.w_emb[y, x, z, c] = v.emb[...]
-    v.small_w[y, x, z, c] = v.small[...]
+    for name in ("emb", "gains", "shifts", "outs", "ubias", "rel"):
+        loads[name].wait()
+    v.small32[...] = jnp.zeros((512, 128), F32)
+    for i, piece in enumerate((v.gains, v.shifts, v.outs, v.ubias, v.rel)):
+        v.small32[i : i + 1, 0 : piece.shape[1]] = piece[...].astype(F32)
+    v.w_emb[y, x, z, c, 0:32] = v.emb[...]
+    v.w_emb[y, x, z, c, 32:48] = v.small32[0:16, :].astype(BF16)
+    pl.semaphore_wait(barrier, len(peers))
+    emb = Direct(net, at, v.w_emb)
+    emb.start()
+
+    loads["qkv"].wait()
     v.lin32[0:192, :] = v.qkv[...].astype(F32)
     for t in range(3):
         for zz in range(4):
             piece = v.lin32[pl.ds(4 * t + zz, 16, stride=12), :].astype(BF16)
             v.qkv_src[zz, :, 128 * t : 128 * t + 128] = piece
     v.w_qkv[y, x, z, c] = v.qkv_src[z]
-    v.lin32[0:64, :] = v.out[...].astype(F32)
-    for j in range(4):
-        v.w_out[y, x, z, c, :, 128 * j : 128 * j + 128] = v.lin32[
-            pl.ds(j, 16, stride=4), :
-        ].astype(BF16)
-    v.lin32[...] = v.up[...].astype(F32)
-    for j in range(16):
-        v.w_up[y, x, z, c, :, 128 * j : 128 * j + 128] = v.lin32[
-            pl.ds(j, 16, stride=16), :
-        ].astype(BF16)
-    v.lin32[...] = v.down[...].astype(F32)
-    for j in range(4):
-        v.w_down[y, x, z, c, :, 128 * j : 128 * j + 128] = v.lin32[
-            pl.ds(j, 64, stride=4), :
-        ].astype(BF16)
-    pl.semaphore_wait(barrier, len(peers))
-
-    emb = Gather(net, at, v.w_emb)
-    small = Gather(net, at, v.small_w)
     qkv = Gather(net, at, v.w_qkv, v.qkv_src)
-    out = Gather(net, at, v.w_out)
-    up = Gather(net, at, v.w_up)
-    down = Gather(net, at, v.w_down)
-    fast, slow = (emb, small, qkv), (out, up, down)
-    for g in fast:
-        g.along_z()
-    for g in slow:
-        g.along_z()
-    for g in fast:
-        g.first()
-    for g in fast:
-        g.second()
+    qkv.along_z()
+    slow = []
+    for name, rows, width in (("out", 16, 4), ("up", 16, 16), ("down", 64, 4)):
+        loads[name].wait()
+        full = getattr(v, "w_" + name)
+        v.lin32[0 : rows * width, :] = getattr(v, name)[...].astype(F32)
+        for j in range(width):
+            full[y, x, z, c, :, 128 * j : 128 * j + 128] = v.lin32[
+                pl.ds(j, rows, stride=width), :
+            ].astype(BF16)
+        slow.append(Relayed(net, at, full))
+        slow[-1].start()
+    out, up, down = slow
+
+    lane = lax.broadcasted_iota(jnp.int32, (128, 512), 1)
+    row = lax.broadcasted_iota(jnp.int32, (128, 512), 0)
+    for i, size in enumerate((32, 64, 8)):
+        v.select[i] = (lax.rem(lane, size) == row).astype(F32).astype(BF16)
+    loads["ids"].wait()
     v.picks[...] = (
         (lax.broadcasted_iota(jnp.int32, (VOCAB, ROWS), 0) == v.ids[...]).astype(F32).astype(BF16)
     )
-    for g in fast:
-        g.cores()
+    emb.cores()
+    qkv.first()
+    loads["stream"].wait()
+    loads["cot"].wait()
     emb.arrive()
-    small.arrive()
-
-    v.small32[...] = v.small_w[...].reshape(256, 128)
-    lane = lax.broadcasted_iota(jnp.int32, (128, 512), 1)
-    row = lax.broadcasted_iota(jnp.int32, (128, 512), 0)
+
+    v.emb32[...] = v.w_emb[:, :, :, :, 0:32, :].reshape(1024, 128).astype(F32)
+    v.small32[...] = v.w_emb[:, :, :, :, 32:48, :].reshape(512, 128).astype(F32)
     owner = lax.broadcasted_iota(jnp.int32, (32, 512), 0)
     where = lax.broadcasted_iota(jnp.int32, (32, 512), 1)
 
-    def tiled(kind, size):
-        pieces = v.small32[pl.ds(kind, 32, stride=8), :].astype(BF16)
-        select = (lax.rem(lane, size) == row).astype(F32).astype(BF16)
-        return dot_nn(pieces, select)
+    def tiled(kind, select):
+        pieces = v.small32[pl.ds(kind, 32, stride=16), :].astype(BF16)
+        return dot_nn(pieces, v.select[select])
 
     def picked(wide, size, first):
         return column_sum(jnp.where(owner == first + lax.div(where, size), wide, 0.0))
 
-    for kind in range(3):
-        wide = tiled(kind, 32)
+    def halves(kind):
+        wide = tiled(kind, 0)
         for half in range(2):
             v.vecs[2 * kind + half : 2 * kind + half + 1, :] = picked(wide, 32, 16 * half)
-    wide = tiled(3, 64)
-    for block in range(4):
-        v.bias_row[:, 512 * block : 512 * block + 512] = picked(wide, 64, 8 * block)
-    rel_row = picked(tiled(4, 8), 8, 0)[:, 0:256]
-    rel_lane = lax.broadcasted_iota(jnp.int32, (1, 256), 1)
-
-    v.emb32[...] = v.w_emb[...].reshape(1024, 128).astype(F32)
+
+    halves(0)
+    halves(1)
     for j in range(4):
         cut = slice(128 * j, 128 * j + 128)
         table = v.emb32[pl.ds(j, VOCAB, stride=4), :].astype(BF16)
@@ -699,9 +913,23 @@
     normed_moves = [None] + [
         net.send(v.normed1.at[z], v.normed1.at[z], at.along_z(s)) for s in (1, 2, 3)
     ]
-
+    qkv.second()
     for g in slow:
-        g.first()
+        g.take_near()
+        g.take_far()
+    halves(2)
+    wide = tiled(3, 1)
+    for block in range(4):
+        v.bias_row[:, 512 * block : 512 * block + 512] = picked(wide, 64, 8 * block)
+    rel_row = picked(tiled(4, 2), 8, 0)[:, 0:256]
+    rel_lane = lax.broadcasted_iota(jnp.int32, (1, 256), 1)
+    qkv.cores()
+    for g in slow:
+        g.second(0)
+    for g in slow:
+        g.take_relay()
+    for g in slow:
+        g.second(1)
 
     qkv.arrive()
     weight = v.w_qkv[...].reshape(512, 384)
@@ -718,7 +946,11 @@
         moves.append(net.send(both, both, at.sibling()))
         if s == 1:
             for g in slow:
-                g.second()
+                g.second(2)
+        if s == 2:
+            for g in slow:
+                g.second(3)
+                g.cores(0)
     for copy in moves:
         copy.wait_recv()
 
@@ -731,6 +963,8 @@
 
     rel_values = [[rel_value(h, d) for d in range(4)] for h in range(2)]
     zero = jnp.zeros((), BF16)
+    own_lanes = pl.ds(pl.multiple_of(z * PAIR, PAIR), PAIR)
+    to_owner = Owners(net, at, lambda k: v.mixed_out.at[k], lambda k: v.mixed.at[:, own_lanes])
     for zq in range(4):
         count = 256 * (zq + 1)
         keys = v.keyval[0, 0 : zq + 1].reshape(count, PAIR)
@@ -751,18 +985,14 @@
             v.probs[h, :, KEYS_AT[zq] : KEYS_AT[zq] + count] = probs
             heads.append(dot_nn(probs.astype(BF16), vals))
         v.mixed_out[zq] = jnp.where(head_lanes[0], heads[0], heads[1]).astype(BF16)
-    own_lanes = pl.ds(pl.multiple_of(z * PAIR, PAIR), PAIR)
-    moves = [
-        net.send(v.mixed_out.at[at.ahead(s)], v.mixed.at[:, own_lanes], at.along_z(s))
-        for s in (1, 2, 3)
-    ]
+        to_owner.send(zq)
     v.mixed[:, own_lanes] = v.mixed_out[z]
-    for g in slow:
-        g.cores()
-    for copy in moves:
-        copy.wait_recv()
-
-    out.arrive()
+    for k in (1, 2, 3):
+        for g in slow:
+            g.cores(k)
+    to_owner.arrive()
+
+    out.done()
     mixed = v.mixed[...]
     out_weight = v.w_out[...].reshape(512, 512)
     middle = v.start[...] + dot_nn(mixed, out_weight) + v.vecs[4:5, :]
@@ -773,52 +1003,55 @@
     v.normed2[...] = (normal * v.vecs[1:2, :] + v.vecs[3:4, :]).astype(BF16)
     v.acc1[...] = jnp.zeros_like(v.acc1)
     v.acc2[...] = jnp.zeros_like(v.acc2)
-    up.arrive()
-    down.arrive()
-
-    def hidden_tile(i, carry):
+    up.done()
+    down.done()
+
+    def scatter(name):
+        bufs = [getattr(v, f"r{i}_{name}") for i in range(6)]
+        return Scatter(net, at, getattr(v, "g_" + name), bufs)
+
+    s_down, s_up, s_out, s_qkv = (scatter(n) for n in ("down", "up", "out", "qkv"))
+    s_emb = DirectScatter(net, at, v.g_emb, v.r0_emb, v.landed)
+
+    def forward_tile(i, carry):
         cols = pl.ds(pl.multiple_of(i * 256, 256), 256)
         ty, tx, tz = lax.div(i, 4), lax.rem(lax.div(i, 2), 2), lax.rem(i, 2) * 2
-        normed = v.normed2[...]
-        grad = v.cot[...]
         up_tile = v.w_up[:, :, :, :, :, cols].reshape(512, 256)
         down_tile = v.w_down[ty, tx, pl.ds(tz, 2)].reshape(256, 512)
-        lifted = dot_nn(normed, up_tile) + v.bias_row[:, cols]
+        lifted = dot_nn(v.normed2[...], up_tile) + v.bias_row[:, cols]
         share = 0.5 * (1.0 + lax.erf(lifted * ROOT_HALF))
         active = (lifted * share).astype(BF16)
-        slope = share + lifted * (jnp.exp(-0.5 * lifted * lifted) * ROOT_TAU)
+        v.slope[:, cols] = share + lifted * (jnp.exp(-0.5 * lifted * lifted) * ROOT_TAU)
         v.acc1[...] += dot_nn(active, down_tile)
-        grad_lifted = dot_nt(grad, down_tile) * slope
+        v.g_down[ty, tx, pl.ds(tz, 2)] = (
+            dot_tn(active, v.cot[...]).astype(BF16).reshape(2, 2, 64, 512)
+        )
+        return carry
+
+    lax.fori_loop(0, 8, forward_tile, 0)
+    s_down.cores()
+
+    def backward_tile(i, carry):
+        cols = pl.ds(pl.multiple_of(i * 256, 256), 256)
+        ty, tx, tz = lax.div(i, 4), lax.rem(lax.div(i, 2), 2), lax.rem(i, 2) * 2
+        up_tile = v.w_up[:, :, :, :, :, cols].reshape(512, 256)
+        down_tile = v.w_down[ty, tx, pl.ds(tz, 2)].reshape(256, 512)
+        grad_lifted = dot_nt(v.cot[...], down_tile) * v.slope[:, cols]
         v.gub[:, cols] = column_sum(grad_lifted)
         low = grad_lifted.astype(BF16)
         v.acc2[...] += dot_nt(low, up_tile)
-        v.g_down[ty, tx, pl.ds(tz, 2)] = dot_tn(active, grad).astype(BF16).reshape(2, 2, 64, 512)
-        v.g_up[:, :, :, :, :, cols] = dot_tn(normed, low).astype(BF16).reshape(2, 2, 4, 2, 16, 256)
+        v.g_up[:, :, :, :, :, cols] = (
+            dot_tn(v.normed2[...], low).astype(BF16).reshape(2, 2, 4, 2, 16, 256)
+        )
         return carry
 
-    lax.fori_loop(0, 8, hidden_tile, 0)
-
-    def scatter(name):
-        bufs = [getattr(v, f"r{i}_{name}") for i in range(6)]
-        return Scatter(net, at, getattr(v, "g_" + name), bufs)
-
-    s_down, s_up, s_out, s_qkv, s_emb = (
-        scatter(n) for n in ("down", "up", "out", "qkv", "emb")
-    )
-    s_down.cores()
+    lax.fori_loop(0, 8, backward_tile, 0)
     s_up.cores()
     grad_wide = v.cot[...].astype(F32)
-    v.act[...] = (v.middle[...] + v.acc1[...] + v.vecs[5:6, :]).astype(BF16)
     upstream = v.acc2[...]
     normal = v.normal2[...]
-    v.sg[1:2, :] = column_sum(upstream * normal)
-    v.sg[3:4, :] = column_sum(upstream)
-    v.sg[5:6, :] = column_sum(grad_wide)
     grad_middle = grad_wide + norm_back(upstream, v.vecs[1:2, :], normal, v.inverse2[...])
     v.grad_mid[...] = grad_middle
-    v.sg[4:5, :] = column_sum(grad_middle)
-    for block in range(4):
-        v.sg[6 + block : 7 + block, :] = v.gub[:, 512 * block : 512 * block + 512]
     middle_low = grad_middle.astype(BF16)
     v.gmix_src[...] = dot_nt(middle_low, v.w_out[...].reshape(512, 512)).astype(BF16)
     moves = [
@@ -833,13 +1066,30 @@
     v.g_out[...] = dot_tn(v.mixed[...], middle_low).astype(BF16).reshape(2, 2, 4, 2, 16, 512)
     s_out.cores()
     s_down.first()
+    v.sg[1:2, :] = column_sum(upstream * normal)
+    v.sg[3:4, :] = column_sum(upstream)
+    v.sg[4:5, :] = column_sum(grad_middle)
+    v.sg[5:6, :] = column_sum(grad_wide)
+    v.act[...] = (v.middle[...] + v.acc1[...] + v.vecs[5:6, :]).astype(BF16)
     s_up.first()
     s_out.first()
     for copy in moves:
         copy.wait_recv()
 
     rel_sums = [[jnp.zeros((1, 256), F32) for d in range(4)] for h in range(2)]
+    weight = v.w_qkv[...].reshape(512, 384)
     core_moves = {}
+    gnorm_out = Owners(net, at, lambda k: v.gnorm.at[k], lambda k: v.gnorm_in.at[z])
+
+    def project_back(zq):
+        core_moves[zq].wait_recv()
+        dkeys = (v.dkv[0, zq, c] + v.dkv_in[0, zq]) * SCALING
+        dvals = v.dkv[1, zq, c] + v.dkv_in[1, zq]
+        v.dproj[zq, :, 128:256] = dkeys.astype(BF16)
+        v.dproj[zq, :, 256:384] = dvals.astype(BF16)
+        v.gnorm[zq] = dot_nt(v.dproj[zq], weight).astype(BF16)
+        gnorm_out.send(zq)
+
     for zq in (3, 2, 1, 0):
         count = 256 * (zq + 1)
         keys = v.keyval[0, 0 : zq + 1].reshape(count, PAIR)
@@ -859,7 +1109,9 @@
             heads.append(dot_nn(low, keys))
             dkeys = dkeys + dot_tn(low, query)
             dvals = dvals + dot_tn(probs.astype(BF16), grad)
-        v.dquery[zq] = (jnp.where(head_lanes[0], heads[0], heads[1]) * SCALING).astype(BF16)
+        v.dproj[zq, :, 0:128] = (
+            jnp.where(head_lanes[0], heads[0], heads[1]) * SCALING
+        ).astype(BF16)
         dkeys = dkeys.reshape(zq + 1, 2, ROWS, PAIR)
         dvals = dvals.reshape(zq + 1, 2, ROWS, PAIR)
         if zq == 3:
@@ -871,32 +1123,21 @@
         core_moves[zq] = net.send(
             v.dkv.at[:, zq, 1 - c], v.dkv_in.at[:, zq], at.sibling()
         )
-        if zq == 2:
+        if zq < 3:
+            project_back(zq + 1)
+        if zq == 1:
             s_down.second()
-            s_up.second()
-            s_out.second()
-    weight = v.w_qkv[...].reshape(512, 384)
-    for zq in (3, 2, 1, 0):
-        core_moves[zq].wait_recv()
-        dkeys = (v.dkv[0, zq, c] + v.dkv_in[0, zq]) * SCALING
-        dvals = v.dkv[1, zq, c] + v.dkv_in[1, zq]
-        v.dproj[zq, :, 0:128] = v.dquery[zq]
-        v.dproj[zq, :, 128:256] = dkeys.astype(BF16)
-        v.dproj[zq, :, 256:384] = dvals.astype(BF16)
-        v.gnorm[zq] = dot_nt(v.dproj[zq], weight).astype(BF16)
-    gnorm_moves = [
-        net.send(v.gnorm.at[at.ahead(s)], v.gnorm_in.at[s - 1], at.along_z(s)) for s in (1, 2, 3)
-    ]
+    project_back(0)
+    s_up.second()
+    s_out.second()
     v.g_qkv[...] = (
         dot_tn(v.normed1[...].reshape(512, 512), v.dproj[...].reshape(512, 384))
         .astype(BF16)
         .reshape(2, 2, 4, 2, 16, 384)
     )
     s_qkv.cores()
-    s_down.along_z()
-    s_up.along_z()
-    s_out.along_z()
-    s_qkv.first()
+    s_down.pair()
+
     sums = jnp.zeros((1, 512), F32)
     wide_lane = lax.broadcasted_iota(jnp.int32, (1, 512), 1)
     for h in range(2):
@@ -904,43 +1145,47 @@
             spot = (2 * z + h) * BUCKETS + d
             value = jnp.sum(rel_sums[h][d], axis=1, keepdims=True)
             sums = sums + jnp.where(wide_lane == spot, value, 0.0)
-    v.sg[10:11, :] = sums
-    v.sg[11:16, :] = jnp.zeros((5, 512), F32)
-
+
+    def cut(kind, select, size, lines):
+        wide = jnp.zeros((32, 512), F32)
+        for i, line in enumerate(lines):
+            first = (512 // size) * i
+            wide = jnp.where(owner == first + lax.div(where, size), line, wide)
+        v.small32[pl.ds(kind, 32, stride=16), :] = dot_nt(wide.astype(BF16), v.select[select])
+
+    v.small32[...] = jnp.zeros((512, 128), F32)
+    cut(2, 0, 32, [v.sg[4:5, :], v.sg[5:6, :]])
+    cut(3, 1, 64, [v.gub[:, 512 * i : 512 * i + 512] for i in range(4)])
+    cut(4, 2, 8, [sums])
+    s_qkv.first()
+
+    gnorm_out.arrive()
     upstream = v.gnorm[z].astype(F32)
-    for s in range(3):
-        gnorm_moves[s].wait_recv()
-        upstream = upstream + v.gnorm_in[s].astype(F32)
+    for s in (1, 2, 3):
+        upstream = upstream + v.gnorm_in[at.ahead(s)].astype(F32)
     normal = v.normal1[...]
-    v.sg[0:1, :] = column_sum(upstream * normal)
-    v.sg[2:3, :] = column_sum(upstream)
     grad_start = v.grad_mid[...] + norm_back(upstream, v.vecs[0:1, :], normal, v.inverse1[...])
     start_low = grad_start.astype(BF16)
-    small_move = net.send(v.sg, v.sg_in.at[0], at.sibling())
-    grad_embed = dot_nn(v.picks[...], start_low)
-    spread(v.emb32, grad_embed, 4)
-    v.g_emb[...] = v.emb32[...].astype(BF16).reshape(2, 2, 4, 2, 32, 128)
+    spread(v.emb32, dot_nn(v.picks[...], start_low), 4)
+    v.g_emb[:, :, :, :, 0:32, :] = v.emb32[...].astype(BF16).reshape(2, 2, 4, 2, 32, 128)
+    cut(0, 0, 32, [column_sum(upstream * normal), v.sg[1:2, :]])
+    cut(1, 0, 32, [column_sum(upstream), v.sg[3:4, :]])
+    v.g_emb[:, :, :, :, 32:48, :] = v.small32[...].astype(BF16).reshape(2, 2, 4, 2, 16, 128)
     s_emb.cores()
     v.gstream[...] = start_low
+    s_up.pair()
+    s_out.pair()
+    s_emb.start()
+    s_down.far()
     s_qkv.second()
-    small_move.wait_recv()
-    v.sg_in[4] = v.sg[...] + v.sg_in[0]
-    small_move = net.send(v.sg_in.at[4], v.sg_in.at[1], at.across_x())
-    s_emb.first()
+    s_up.far()
+    s_out.far()
+    s_qkv.along_z()
     spread(v.o_down, s_down.total(), 4)
-    small_move.wait_recv()
-    v.sg_in[5] = v.sg_in[4] + v.sg_in[1]
-    small_move = net.send(v.sg_in.at[5], v.sg_in.at[2], at.across_y())
-    s_qkv.along_z()
-    s_emb.second()
+    total = s_emb.total()
+    v.o_emb[...] = total[0:32]
+    v.o_small[...] = total[32:40]
     spread(v.o_up, s_up.total(), 16)
-    small_move.wait_recv()
-    total = v.sg_in[5] + v.sg_in[2]
-    v.sg_in[3] = total
-    small_moves = [
-        net.send(v.sg_in.at[3], v.small_z.at[s - 1], at.along_z(s)) for s in (1, 2, 3)
-    ]
-    s_emb.along_z()
     spread(v.o_out, s_out.total(), 4)
     s_qkv.arrive()
     v.gathered[z] = v.r0_qkv[y, x, z]
@@ -950,24 +1195,20 @@
         piece = v.gathered[zz].astype(F32)
         for t in range(3):
             v.o_qkv[pl.ds(4 * t + zz, 16, stride=12), :] = piece[:, 128 * t : 128 * t + 128]
-    for s in range(3):
-        small_moves[s].wait_recv()
-        total = total + v.small_z[s]
-    v.sg_total[...] = total
-
-    def shard(row_at, offset):
-        line = jnp.broadcast_to(v.sg_total[pl.ds(row_at, 1), :], (8, 512))
-        return pltpu.roll(line, lax.rem(512 - offset, 512), 1)[0:1, 0:128]
-
-    line = 32 * lax.rem(at.flat, 16)
-    v.o_small[0:1, :] = shard(y, line)
-    v.o_small[1:2, :] = shard(2 + y, line)
-    v.o_small[2:3, :] = shard(4 + y, line)
-    v.o_small[3:4, :] = shard(6 + at.dp, 64 * at.seq)
-    v.o_small[4:5, :] = shard(10, 8 * at.flat)
-    v.o_small[5:8, :] = jnp.zeros((3, 128), F32)
-    v.o_emb[...] = s_emb.total()
+    to_owner.drain()
+    gnorm_out.drain()
     net.drain()
+
+
+def store_kernel(*refs):
+    ins, small, outs, sems = refs[:7], refs[7], refs[8:20], refs[20]
+    copies = [pltpu.make_async_copy(ins[i], outs[i], sems.at[i]) for i in range(7)]
+    for copy in copies:
+        copy.start()
+    for i in range(5):
+        outs[7 + i][...] = small[i : i + 1, 0 : outs[7 + i].shape[1]]
+    for copy in copies:
+        copy.wait()
 
 
 def fused_local(
@@ -985,13 +1226,6 @@
     up_bias,
     rel_bias,
 ):
-    def line(piece):
-        return jnp.pad(piece.astype(F32), (0, 128 - piece.shape[0]))[None]
-
-    small = jnp.concatenate(
-        [line(p) for p in (gains, norm_shifts, out_shifts, up_bias, rel_bias)]
-        + [jnp.zeros((3, 128), F32)]
-    )
     operands = (
         stream.reshape(ROWS, D),
         byte_ids,
@@ -1001,7 +1235,11 @@
         out_flat.reshape(-1, 128),
         up_flat.reshape(-1, 128),
         down_flat.reshape(-1, 128),
-        small,
+        gains.reshape(1, -1),
+        norm_shifts.reshape(1, -1),
+        out_shifts.reshape(1, -1),
+        up_bias.reshape(1, -1),
+        rel_bias.reshape(1, -1),
     )
     shapes = (
         ((ROWS, D), BF16),
@@ -1014,30 +1252,33 @@
         ((8, 128), F32),
     )
     whole = pl.BlockSpec(memory_space=pltpu.VMEM)
-    act, gstream, g_emb, g_qkv, g_out, g_up, g_down, g_small = pl.pallas_call(
+    anywhere = pl.BlockSpec(memory_space=pl.ANY)
+    results = pl.pallas_call(
         fused_kernel,
         out_shape=[jax.ShapeDtypeStruct(s, t) for s, t in shapes],
-        in_specs=[whole] * len(operands),
+        in_specs=[pl.BlockSpec(memory_space=pltpu.HBM)] * len(operands),
         out_specs=[whole] * len(shapes),
         scratch_shapes=list(scratch().values()),
         compiler_params=pltpu.CompilerParams(
-            collective_id=0, has_side_effects=True, vmem_limit_bytes=60 << 20
+            collective_id=0, has_side_effects=True, vmem_limit_bytes=32 << 20
         ),
         name="layer",
     )(*operands)
+    vectors = (gains, norm_shifts, out_shifts, up_bias, rel_bias)
+    small_shapes = [((1, p.shape[0]), F32) for p in vectors]
+    final = pl.pallas_call(
+        store_kernel,
+        out_shape=[jax.ShapeDtypeStruct(s, t) for s, t in shapes[:7] + tuple(small_shapes)],
+        in_specs=[whole] * 8,
+        out_specs=[anywhere] * 7 + [whole] * 5,
+        scratch_shapes=[pltpu.SemaphoreType.DMA((7,))],
+        compiler_params=pltpu.CompilerParams(vmem_limit_bytes=8 << 20),
+        name="store",
+    )(*results)
     return (
-        act.reshape(stream.shape),
-        gstream.reshape(stream.shape),
-        g_emb.reshape(-1),
-        g_qkv.reshape(-1),
-        g_out.reshape(-1),
-        g_up.reshape(-1),
-        g_down.reshape(-1),
-        g_small[0, : gains.shape[0]],
-        g_small[1, : norm_shifts.shape[0]],
-        g_small[2, : out_shifts.shape[0]],
-        g_small[3, : up_bias.shape[0]],
-        g_small[4, : rel_bias.shape[0]],
+        final[0].reshape(stream.shape),
+        final[1].reshape(stream.shape),
+        *(part.reshape(-1) for part in final[2:]),
     )
 
 

time: 124 us -> 104 us (0.84)
  Pallas kernels: 110 us -> 97.2 us
  local copies, waits for them, and re-layouts: 11.6 us -> 5.66 us
    pallas_call x1, Pallas kernels: 110 us -> 95.8 us  [fused_local(): pl.pallas_call(fused_kernel, out_shape=[jax.ShapeDtypeStruct(s, t) for s,...]
    squeeze x3 -> x0, local copies, waits for them, and re-layouts: 3.7 us -> none  [the longest x1 1.32 us: fused_local(): g_small[2, :out_shifts.shape[0]]]
    unnamed x25 -> x26, local copies, waits for them, and re-layouts: 7.25 us -> 5.66 us
    pallas_call x0 -> x1, Pallas kernels: none -> 1.43 us  [fused_local(): pl.pallas_call(store_kernel, out_shape=[jax.ShapeDtypeStruct(s, t) for s,...]
where the time goes in v2:
time: 104 us
  Pallas kernels  97.2 us (93%)
  local copies, waits for them, and re-layouts  5.66 us (5%)
    pallas_call x1, Pallas kernels, fused_local(): pl.pallas_call(fused_kernel, out_shape=[jax.ShapeDtypeStruct(s, t) for s,...  95.8 us
    unnamed x26, local copies, waits for them, and re-layouts  5.66 us

profile of v2, /device:TPU:0, one launch (start us, length us, event | category | flops | bytes accessed | tf_op | source)
XLA Modules:
  0.0 103.6 jit_solution(12660166253785406939)
XLA Ops:
  0.6 0.0 copy-start.5
  0.7 0.0 copy-start.10
  0.7 0.0 copy-start.11
  0.7 0.0 copy-start.12
  0.7 0.0 copy-start.7
  0.7 0.0 copy-start.8
  0.7 0.0 copy-start.9
  0.7 0.6 copy-done.5
  1.4 0.0 copy-done.10
  1.4 0.0 copy-done.11
  1.4 0.0 copy-done.12
  1.4 0.0 copy-done.7
  1.4 0.0 copy-done.8
  1.4 0.0 copy-done.9
  1.4 0.0 copy-start
  1.4 0.9 copy-done
  2.3 0.0 copy-start.1
  2.3 0.9 copy-done.1
  3.2 0.0 copy-start.2
  3.2 0.8 copy-done.2
  4.1 0.0 copy-start.3
  4.1 0.8 copy-done.3
  4.9 0.0 copy-start.4
  4.9 0.8 copy-done.4
  5.7 0.0 copy-start.6
  5.7 0.7 copy-done.6
  6.4 95.8 %layer.1 = (bf16[128,512]{1,0:T(8,128)(2,1)S(1)}, bf16[128,512]{1,0:T(8,128)(2,1)S(1)}, f32[32,128]{1,0:T(8,128)S(1)}, f32[192,128]{1,0:T(8,128)S(1)}, f32[64,12...) custom-call(bf16[128,512]{1,0:T(8,128)(2,1)S(1)} %bitcast.24, ...), custom_call_target="tpu_custom_call" | custom-call | tf_op jit(solution)/shard_map/layer/pallas_call | solution.py:1256
  102.2 1.4 %store.1 = (bf16[128,512]{1,0:T(8,128)(2,1)}, bf16[128,512]{1,0:T(8,128)(2,1)}, f32[32,128]{1,0:T(8,128)}, f32[192,128]{1,0:T(8,128)}, f32[64,128]{1,0:T(8,128)}...) custom-call(bf16[128,512]{1,0:T(8,128)(2,1)S(1)} %get-tuple-element., ...), custom_call_target="tpu_custom_call" | custom-call | tf_op jit(solution)/shard_map/store/pallas_call | solution.py:1269
Async XLA Ops:
  0.6 0.7 copy-start.5
  0.7 0.7 copy-start.10
  0.7 0.7 copy-start.11
  0.7 0.7 copy-start.12
  0.7 0.7 copy-start.7
  0.7 0.7 copy-start.8
  0.7 0.7 copy-start.9
  1.4 0.9 copy-start
  2.3 0.9 copy-start.1
  3.2 0.8 copy-start.2
  4.1 0.8 copy-start.3
  4.9 0.8 copy-start.4
  5.7 0.7 copy-start.6

commit v3 on v2

--- a/solution.py
+++ b/solution.py
@@ -412,6 +412,13 @@
     def across_y(self):
         return self.dev(1 - self.y, self.x, self.z, self.c)
 
+    def across_xy(self):
+        return self.dev(1 - self.y, 1 - self.x, self.z, self.c)
+
+    def line(self):
+        near = self.near()
+        return self.z, near, self.ahead(2), lax.rem(near + 2, 4)
+
     def near(self):
         return self.z + 1 - 2 * lax.rem(self.z, 2)
 
@@ -438,41 +445,27 @@
         return self.dev(self.y, self.x, self.ahead(step), self.c)
 
 
-class Gather:
-    def __init__(self, net, at, full, sources=None):
+class Columns:
+    def __init__(self, net, at, full, sources):
         self.net, self.at, self.full, self.sources = net, at, full, sources
 
     def along_z(self):
         at = self.at
         own = self.full.at[at.y, at.x, at.z, at.c]
-        self.waits = []
-        for step in (1, 2, 3):
-            src = own if self.sources is None else self.sources.at[at.ahead(step)]
-            self.waits.append(self.net.send(src, own, at.along_z(step)))
+        self.waits = [
+            self.net.send(self.sources.at[at.ahead(s)], own, at.along_z(s)) for s in (2, 1, 3)
+        ]
 
     def arrive(self):
         for copy in self.waits:
             copy.wait_recv()
 
-    def first(self):
+    def plane(self):
         self.arrive()
-        at, full = self.at, self.full
-        low = full.at[at.y, at.x, 0:2, at.c]
-        high = full.at[at.y, at.x, 2:4, at.c]
-        self.waits = [
-            self.net.send(low, low, at.across_x()),
-            self.net.send(high, high, at.across_y()),
-        ]
-
-    def second(self):
-        self.arrive()
-        at, full = self.at, self.full
-        low = full.at[at.y, :, 0:2, at.c]
-        high = full.at[:, at.x, 2:4, at.c]
-        self.waits = [
-            self.net.send(low, low, at.across_y()),
-            self.net.send(high, high, at.across_x()),
-        ]
+        at = self.at
+        blocks = self.full.at[at.y, at.x, :, at.c]
+        peers = (at.across_xy(), at.across_x(), at.across_y())
+        self.waits = [self.net.send(blocks, blocks, peer) for peer in peers]
 
     def cores(self):
         self.arrive()
@@ -530,52 +523,43 @@
 class Relayed:
     def __init__(self, net, at, full):
         self.net, self.at, self.full = net, at, full
-        far = at.ahead(2)
-        near = at.near()
-        self.zs = (at.z, near, far, lax.rem(near + 2, 4))
-        self.firsts, self.seconds, self.core_moves = [None] * 4, [None] * 4, [None] * 4
+        self.zs = at.line()
+        self.planes, self.core_moves = [None] * 4, [None] * 4
 
     def block(self, z):
         at = self.at
         return self.full.at[at.y, at.x, z, at.c]
 
-    def first(self, k):
-        at = self.at
-        block = self.block(self.zs[k])
-        self.firsts[k] = self.net.send(block, block, at.across_y() if k % 2 else at.across_x())
-
-    def start(self):
-        at = self.at
-        own = self.block(at.z)
-        self.far = self.net.send(own, own, at.toward(self.zs[2]))
-        self.near = self.net.send(own, own, at.toward(self.zs[1]))
-        self.first(0)
+    def plane(self, k):
+        at, block = self.at, self.block(self.zs[k])
+        peers = (at.across_xy(), at.across_x(), at.across_y())
+        self.planes[k] = [self.net.send(block, block, peer) for peer in peers]
+
+    def send_near(self):
+        own = self.block(self.at.z)
+        self.near = self.net.send(own, own, self.at.toward(self.zs[1]))
+
+    def send_far(self):
+        own = self.block(self.at.z)
+        self.far = self.net.send(own, own, self.at.toward(self.zs[2]))
 
     def take_near(self):
         self.near.wait_recv()
-        self.first(1)
+        self.plane(1)
 
     def take_far(self):
         self.far.wait_recv()
         block = self.block(self.zs[2])
         self.relay = self.net.send(block, block, self.at.toward(self.zs[1]))
-        self.first(2)
+        self.plane(2)
 
     def take_relay(self):
         self.relay.wait_recv()
-        self.first(3)
-
-    def second(self, k):
-        self.firsts[k].wait_recv()
-        at, z = self.at, self.zs[k]
-        if k % 2:
-            blocks, peer = self.full.at[:, at.x, z, at.c], at.across_x()
-        else:
-            blocks, peer = self.full.at[at.y, :, z, at.c], at.across_y()
-        self.seconds[k] = self.net.send(blocks, blocks, peer)
+        self.plane(3)
 
     def cores(self, k):
-        self.seconds[k].wait_recv()
+        for copy in self.planes[k]:
+            copy.wait_recv()
         blocks = self.full.at[:, :, self.zs[k], self.at.c]
         self.core_moves[k] = self.net.send(blocks, blocks, self.at.sibling())
 
@@ -740,6 +724,7 @@
     "ubias",
     "rel",
 ]
+LOADS = INPUTS[3:4] + INPUTS[8:] + INPUTS[4:8] + INPUTS[0:3]
 OUTPUTS = ["act", "gstream", "o_emb", "o_qkv", "o_out", "o_up", "o_down", "o_small"]
 
 
@@ -778,6 +763,7 @@
         dkv=vm((2, 4, 2, 128, 128), F32),
         dkv_in=vm((2, 4, 128, 128), F32),
         slope=vm((128, 2048), F32),
+        active=vm((128, 2048), BF16),
         dproj=vm((4, 128, 384), BF16),
         gnorm=vm((4, 128, 512), BF16),
         gnorm_in=vm((4, 128, 512), BF16),
@@ -823,18 +809,18 @@
     net = Net(v.send_sems, v.recv_sems)
     y, x, z, c = at.y, at.x, at.z, at.c
 
-    loads = {}
-    for i, name in enumerate(INPUTS):
-        loads[name] = pltpu.make_async_copy(
-            getattr(v, "h_" + name), getattr(v, name), v.in_sems.at[i]
-        )
-        loads[name].start()
     barrier = pltpu.get_barrier_semaphore()
     peers = [at.dev(*at.other(*way), c) for way in at.others()] + [at.sibling()]
     for peer in peers:
         pl.semaphore_signal(
             barrier, inc=1, device_id=peer, device_id_type=pl.DeviceIdType.MESH
         )
+    loads = {}
+    for i, name in enumerate(LOADS):
+        loads[name] = pltpu.make_async_copy(
+            getattr(v, "h_" + name), getattr(v, name), v.in_sems.at[i]
+        )
+        loads[name].start()
 
     for name in ("emb", "gains", "shifts", "outs", "ubias", "rel"):
         loads[name].wait()
@@ -854,7 +840,7 @@
             piece = v.lin32[pl.ds(4 * t + zz, 16, stride=12), :].astype(BF16)
             v.qkv_src[zz, :, 128 * t : 128 * t + 128] = piece
     v.w_qkv[y, x, z, c] = v.qkv_src[z]
-    qkv = Gather(net, at, v.w_qkv, v.qkv_src)
+    qkv = Columns(net, at, v.w_qkv, v.qkv_src)
     qkv.along_z()
     slow = []
     for name, rows, width in (("out", 16, 4), ("up", 16, 16), ("down", 64, 4)):
@@ -866,7 +852,10 @@
                 pl.ds(j, rows, stride=width), :
             ].astype(BF16)
         slow.append(Relayed(net, at, full))
-        slow[-1].start()
+        if name != "down":
+            slow[-1].send_near()
+            slow[-1].send_far()
+        slow[-1].plane(0)
     out, up, down = slow
 
     lane = lax.broadcasted_iota(jnp.int32, (128, 512), 1)
@@ -878,7 +867,6 @@
         (lax.broadcasted_iota(jnp.int32, (VOCAB, ROWS), 0) == v.ids[...]).astype(F32).astype(BF16)
     )
     emb.cores()
-    qkv.first()
     loads["stream"].wait()
     loads["cot"].wait()
     emb.arrive()
@@ -910,47 +898,60 @@
     v.normal1[...] = normal
     v.inverse1[...] = inverse
     v.normed1[z] = (normal * v.vecs[0:1, :] + v.vecs[2:3, :]).astype(BF16)
-    normed_moves = [None] + [
-        net.send(v.normed1.at[z], v.normed1.at[z], at.along_z(s)) for s in (1, 2, 3)
+    line = at.line()
+    own = v.normed1.at[z]
+    halves_of = [pl.ds(0, 64), pl.ds(64, 64)]
+    normed_near = net.send(own, own, at.toward(line[1]))
+    normed_far = [
+        net.send(v.normed1.at[z, part], v.normed1.at[z, part], at.toward(line[2]))
+        for part in halves_of
     ]
-    qkv.second()
-    for g in slow:
-        g.take_near()
-        g.take_far()
+    qkv.plane()
+    out.take_near()
+    up.take_near()
     halves(2)
     wide = tiled(3, 1)
     for block in range(4):
         v.bias_row[:, 512 * block : 512 * block + 512] = picked(wide, 64, 8 * block)
     rel_row = picked(tiled(4, 2), 8, 0)[:, 0:256]
     rel_lane = lax.broadcasted_iota(jnp.int32, (1, 256), 1)
+    out.take_far()
+    up.take_far()
+    down.send_near()
+    for g in (out, up, down):
+        g.cores(0)
     qkv.cores()
-    for g in slow:
-        g.second(0)
-    for g in slow:
-        g.take_relay()
-    for g in slow:
-        g.second(1)
 
     qkv.arrive()
     weight = v.w_qkv[...].reshape(512, 384)
     moves = []
-    for s in range(4):
-        if s:
-            normed_moves[s].wait_recv()
-        zs = at.behind(s)
+
+    def project(zs):
         projected = dot_nn(v.normed1[zs], weight).astype(BF16)
         v.query[zs] = projected[:, 0:128]
         v.keyval[0, zs, c] = projected[:, 128:256]
         v.keyval[1, zs, c] = projected[:, 256:384]
         both = v.keyval.at[:, zs, c]
         moves.append(net.send(both, both, at.sibling()))
-        if s == 1:
-            for g in slow:
-                g.second(2)
-        if s == 2:
-            for g in slow:
-                g.second(3)
-                g.cores(0)
+
+    project(z)
+    normed_relay = []
+    for i, part in enumerate(halves_of):
+        normed_far[i].wait_recv()
+        piece = v.normed1.at[line[2], part]
+        normed_relay.append(net.send(piece, piece, at.toward(line[1])))
+    down.send_far()
+    normed_near.wait_recv()
+    project(line[1])
+    project(line[2])
+    out.take_relay()
+    up.take_relay()
+    out.cores(1)
+    up.cores(1)
+    for copy in normed_relay:
+        copy.wait_recv()
+    project(line[3])
+    down.take_near()
     for copy in moves:
         copy.wait_recv()
 
@@ -987,9 +988,12 @@
         v.mixed_out[zq] = jnp.where(head_lanes[0], heads[0], heads[1]).astype(BF16)
         to_owner.send(zq)
     v.mixed[:, own_lanes] = v.mixed_out[z]
-    for k in (1, 2, 3):
-        for g in slow:
-            g.cores(k)
+    for k in (2, 3):
+        out.cores(k)
+        up.cores(k)
+    down.take_far()
+    down.cores(1)
+    down.take_relay()
     to_owner.arrive()
 
     out.done()
@@ -1003,8 +1007,8 @@
     v.normed2[...] = (normal * v.vecs[1:2, :] + v.vecs[3:4, :]).astype(BF16)
     v.acc1[...] = jnp.zeros_like(v.acc1)
     v.acc2[...] = jnp.zeros_like(v.acc2)
+    down.cores(2)
     up.done()
-    down.done()
 
     def scatter(name):
         bufs = [getattr(v, f"r{i}_{name}") for i in range(6)]
@@ -1017,25 +1021,27 @@
         cols = pl.ds(pl.multiple_of(i * 256, 256), 256)
         ty, tx, tz = lax.div(i, 4), lax.rem(lax.div(i, 2), 2), lax.rem(i, 2) * 2
         up_tile = v.w_up[:, :, :, :, :, cols].reshape(512, 256)
-        down_tile = v.w_down[ty, tx, pl.ds(tz, 2)].reshape(256, 512)
         lifted = dot_nn(v.normed2[...], up_tile) + v.bias_row[:, cols]
         share = 0.5 * (1.0 + lax.erf(lifted * ROOT_HALF))
         active = (lifted * share).astype(BF16)
+        v.active[:, cols] = active
         v.slope[:, cols] = share + lifted * (jnp.exp(-0.5 * lifted * lifted) * ROOT_TAU)
-        v.acc1[...] += dot_nn(active, down_tile)
         v.g_down[ty, tx, pl.ds(tz, 2)] = (
             dot_tn(active, v.cot[...]).astype(BF16).reshape(2, 2, 64, 512)
         )
         return carry
 
-    lax.fori_loop(0, 8, forward_tile, 0)
+    lax.fori_loop(0, 8, forward_tile, 0, unroll=2)
     s_down.cores()
+    down.cores(3)
+    down.done()
 
     def backward_tile(i, carry):
         cols = pl.ds(pl.multiple_of(i * 256, 256), 256)
         ty, tx, tz = lax.div(i, 4), lax.rem(lax.div(i, 2), 2), lax.rem(i, 2) * 2
         up_tile = v.w_up[:, :, :, :, :, cols].reshape(512, 256)
         down_tile = v.w_down[ty, tx, pl.ds(tz, 2)].reshape(256, 512)
+        v.acc1[...] += dot_nn(v.active[:, cols], down_tile)
         grad_lifted = dot_nt(v.cot[...], down_tile) * v.slope[:, cols]
         v.gub[:, cols] = column_sum(grad_lifted)
         low = grad_lifted.astype(BF16)
@@ -1045,7 +1051,9 @@
         )
         return carry
 
-    lax.fori_loop(0, 8, backward_tile, 0)
+    lax.fori_loop(0, 4, backward_tile, 0, unroll=2)
+    s_down.first()
+    lax.fori_loop(4, 8, backward_tile, 0, unroll=2)
     s_up.cores()
     grad_wide = v.cot[...].astype(F32)
     upstream = v.acc2[...]
@@ -1065,7 +1073,6 @@
     v.gmix[z] = v.gmix_src[:, own_lanes]
     v.g_out[...] = dot_tn(v.mixed[...], middle_low).astype(BF16).reshape(2, 2, 4, 2, 16, 512)
     s_out.cores()
-    s_down.first()
     v.sg[1:2, :] = column_sum(upstream * normal)
     v.sg[3:4, :] = column_sum(upstream)
     v.sg[4:5, :] = column_sum(grad_middle)
@@ -1125,7 +1132,7 @@
         )
         if zq < 3:
             project_back(zq + 1)
-        if zq == 1:
+        if zq == 3:
             s_down.second()
     project_back(0)
     s_up.second()
@@ -1137,6 +1144,8 @@
     )
     s_qkv.cores()
     s_down.pair()
+    s_up.pair()
+    s_out.pair()
 
     sums = jnp.zeros((1, 512), F32)
     wide_lane = lax.broadcasted_iota(jnp.int32, (1, 512), 1)
@@ -1173,8 +1182,6 @@
     v.g_emb[:, :, :, :, 32:48, :] = v.small32[...].astype(BF16).reshape(2, 2, 4, 2, 16, 128)
     s_emb.cores()
     v.gstream[...] = start_low
-    s_up.pair()
-    s_out.pair()
     s_emb.start()
     s_down.far()
     s_qkv.second()
@@ -1255,7 +1262,7 @@
     anywhere = pl.BlockSpec(memory_space=pl.ANY)
     results = pl.pallas_call(
         fused_kernel,
-        out_shape=[jax.ShapeDtypeStruct(s, t) for s, t in shapes],
+        out_shape=[pltpu.VMEM(s, t) for s, t in shapes],
         in_specs=[pl.BlockSpec(memory_space=pltpu.HBM)] * len(operands),
         out_specs=[whole] * len(shapes),
         scratch_shapes=list(scratch().values()),
@@ -1263,7 +1270,7 @@
             collective_id=0, has_side_effects=True, vmem_limit_bytes=32 << 20
         ),
         name="layer",
-    )(*operands)
+    )(*(pltpu.with_memory_space_constraint(o, pltpu.HBM) for o in operands))
     vectors = (gains, norm_shifts, out_shifts, up_bias, rel_bias)
     small_shapes = [((1, p.shape[0]), F32) for p in vectors]
     final = pl.pallas_call(

time: 104 us -> 92.2 us (0.89)
  Pallas kernels: 97.2 us -> 91.2 us
  local copies, waits for them, and re-layouts: 5.66 us -> 0 us
    pallas_call x1, Pallas kernels: 95.8 us -> 89.7 us  [fused_local(): pl.pallas_call(fused_kernel, out_shape=[pltpu.VMEM(s, t) for s, t in shap...]
    unnamed x26 -> x0, local copies, waits for them, and re-layouts: 5.66 us -> none
where the time goes in v3:
time: 92.2 us; the launch traced here: 92 us
  Pallas kernels  91.2 us (99%)
    pallas_call x1, Pallas kernels, fused_local(): pl.pallas_call(fused_kernel, out_shape=[pltpu.VMEM(s, t) for s, t in shap...  89.7 us

profile of v3, /device:TPU:0, one launch (start us, length us, event | category | flops | bytes accessed | tf_op | source)
XLA Modules:
  0.0 92.0 jit_solution(16785839895942986900)
XLA Ops:
  0.6 89.7 %layer.1 = (bf16[128,512]{1,0:T(8,128)(2,1)S(1)}, bf16[128,512]{1,0:T(8,128)(2,1)S(1)}, f32[32,128]{1,0:T(8,128)S(1)}, f32[192,128]{1,0:T(8,128)S(1)}, f32[64,12...) custom-call(bf16[128,512]{1,0:T(8,128)(2,1)} %bitcast.24, ...), custom_call_target="tpu_custom_call" | custom-call | tf_op jit(solution)/shard_map/layer/pallas_call | solution.py:1263
  90.4 1.4 %store.1 = (bf16[128,512]{1,0:T(8,128)(2,1)}, bf16[128,512]{1,0:T(8,128)(2,1)}, f32[32,128]{1,0:T(8,128)}, f32[192,128]{1,0:T(8,128)}, f32[64,128]{1,0:T(8,128)}...) custom-call(bf16[128,512]{1,0:T(8,128)(2,1)S(1)} %get-tuple-element., ...), custom_call_target="tpu_custom_call" | custom-call | tf_op jit(solution)/shard_map/store/pallas_call | solution.py:1276
